TPU v7x, 32 devices: a whole 2x2x4 slice. The times are simulated.
32 devices in a mesh: dp: 8 (over y, x, core), tensor: 4 (over z).
Axes of the slice: x: 2, y: 2, z: 4, core: 2. Of those that a mesh axis runs over, the one named last changes fastest.
Arguments:
- short_tokens: bfloat16 [16, 256, 768], P('dp'), may hold values from -6 to 6
- short_lengths: int32 [16], P('dp'), may hold values from 64 to 256, as said below
- long_tokens: bfloat16 [24, 512, 768], P('dp'), may hold values from -6 to 6
- long_lengths: int32 [24], P('dp'), may hold values from 257 to 512, as said below
- w_qkv: bfloat16 [3, 768, 768], P(None, None, 'tensor'), may hold values from -0.21875 to 0.21875
- b_qv: bfloat16 [2, 12, 64], P(None, 'tensor'), may hold values from -3 to 3
- w_out: bfloat16 [768, 768], P('tensor'), may hold values from -2.5 to 2.5
- res_biases: bfloat16 [2, 768], replicated, may hold values from -3 to 3
- ln_gains: bfloat16 [2, 768], replicated, may hold values from 0.099609375 to 1.8984375
- ln_shifts: bfloat16 [2, 768], replicated, may hold values from -3 to 3
- w_up: bfloat16 [768, 3072], P(None, 'tensor'), may hold values from -0.21875 to 0.21875
- b_up: bfloat16 [4, 768], P('tensor'), may hold values from -3 to 3
- w_down: bfloat16 [3072, 768], P('tensor'), may hold values from -0.109375 to 0.109375
- short_cotangent: bfloat16 [16, 256, 768], P('dp'), may hold values from -6 to 6
- long_cotangent: bfloat16 [24, 512, 768], P('dp'), may hold values from -6 to 6
Outputs:
- short_encoded: bfloat16 [16, 256, 768], P('dp')
- long_encoded: bfloat16 [24, 512, 768], P('dp')
- short_grad_tokens: float32 [16, 256, 768], P('dp')
- long_grad_tokens: float32 [24, 512, 768], P('dp')
- grad_qkv: float32 [3, 768, 768], P(None, 'dp', 'tensor')
- grad_qv_bias: float32 [2, 12, 64], P(None, 'tensor', 'dp')
- grad_out: float32 [768, 768], P('tensor', 'dp')
- grad_res_biases: float32 [2, 768], P(None, 'dp')
- grad_gains: float32 [2, 768], P(None, 'dp')
- grad_shifts: float32 [2, 768], P(None, 'dp')
- grad_up: float32 [768, 3072], P('dp', 'tensor')
- grad_up_bias: float32 [4, 768], P('tensor', 'dp')
- grad_down: float32 [3072, 768], P('tensor', 'dp')
Inputs may be any that keep to these rules, and one draw needn't show every extreme that they name: `short_lengths`: the first short pair has 256 valid tokens. `long_lengths`: the first long pair has 512 valid tokens.
All inputs are finite; a program needn't handle non-finite values.
Results may differ from a plain program's by a relative error of at most 0.013.
The roundings to bfloat16 on the way count: a program that leaves them out, or rounds other values in their place, can miss the bound.
Values sent between devices are 32-bit elements; how exact they have to be, the bound alone decides.
No kernel may reach another device: no remote copies, remote signals or barrier semaphores. Data moves between devices by JAX's collectives and lax.ppermute only.
A program may use at most 128 MiB of HBM per device.

v0:
```python
import jax
import jax.numpy as jnp
import numpy as np
from jax import lax
from jax.experimental import pallas as pl
from jax.experimental.pallas import tpu as pltpu
from jax.sharding import PartitionSpec as P

HD = 64
EPS = 1e-12
BF = jnp.bfloat16
F32 = jnp.float32
NT = (((1,), (1,)), ((), ()))
TN = (((0,), (0,)), ((), ()))


def dot(a, b, dims=(((1,), (0,)), ((), ()))):
    return lax.dot_general(a, b, dims, preferred_element_type=F32)


def lanes(width, test):
    lane = lax.broadcasted_iota(jnp.int32, (1, width), 1)
    return jnp.where(test(lane), 1.0, 0.0).astype(F32)


def head_row(h, width, extra):
    w = width * HD

    def test(lane):
        own = (lane >= h * HD) & (lane < (h + 1) * HD)
        if extra:
            own = own | ((lane >= w + 1 + 3 * h) & (lane < w + 4 + 3 * h))
        return own

    return test


def split3(x):
    hi = x.astype(BF).astype(F32)
    rest = x - hi
    mid = rest.astype(BF).astype(F32)
    return hi, mid, rest - mid


def blocks(blk, d, nshort, grid_pos=0):
    return [
        pl.BlockSpec((blk, d), lambda *g: (jnp.minimum(g[grid_pos], nshort - 1), 0)),
        pl.BlockSpec((blk, d), lambda *g: (jnp.maximum(g[grid_pos] - nshort, 0), 0)),
    ]


def fetch(jobs, stage, sems, depth):
    def copy(n):
        src, idx, _ = jobs[n]
        dst = stage.at[n % depth] if idx is None else stage.at[n % depth, idx]
        return pltpu.make_async_copy(src, dst, sems.at[n % depth])

    for n in range(min(depth - 1, len(jobs))):
        copy(n).start()
    for n in range(len(jobs)):
        if n + depth - 1 < len(jobs):
            copy(n + depth - 1).start()
        copy(n).wait()
        jobs[n][2](n % depth)


def attn_fwd_kernel(
    len_ref, place_ref, xs_ref, xl_ref, b_ref, *refs, slot, nshort, short_slot, heads, blk
):
    if slot:
        pieces, (p_ref, o_ref, w_s, x_s, stage, sems) = refs[:8], refs[-6:]
    else:
        w_ref, p_ref, o_ref, w_s, x_s = refs
    hw = heads * HD
    b = pl.program_id(0)
    sub = blk // short_slot
    long0 = nshort // sub

    @pl.when(b == 0)
    def _():
        if slot:
            copies = [
                pltpu.make_async_copy(pieces[n].at[slot - 1], stage.at[n], sems.at[n])
                for n in range(8)
            ]
            for c in copies:
                c.start()
            w_s[...] = jnp.zeros_like(w_s)
            r = stage.shape[1]
            for n in range(8):
                copies[n].wait()
                row = place_ref[1, n]

                @pl.when(row >= 0)
                def _():
                    w_s[pl.ds(pl.multiple_of(row, 32), r)] = stage[n].astype(BF)

        else:
            w_s[...] = jnp.zeros_like(w_s)
            for c in range(3):
                w_s[256 * c : 256 * c + hw] = w_ref[c * hw : (c + 1) * hw]

    @pl.when(b < long0)
    def _():
        x_s[...] = xs_ref[...]

    @pl.when(b >= long0)
    def _():
        x_s[...] = xl_ref[...]

    p_ref[0] = (dot(x_s[...], w_s[...], NT) + b_ref[...]).astype(BF)

    def pair(row, rows, length):
        sl = pl.ds(row, rows)
        pos = lax.broadcasted_iota(jnp.int32, (rows, 1), 0)
        hidden = jnp.where(pos < length, 0.0, -1e30)
        at_mask = lanes(256, lambda l: l == hw)
        q = (p_ref[0, sl, 0:256].astype(F32) * 0.125 + at_mask).astype(BF)
        k = (p_ref[0, sl, 256:512].astype(F32) + hidden * at_mask).astype(BF)
        v = p_ref[0, sl, 512:768]
        p_ref[0, sl, 256:512] = k
        out = jnp.zeros((rows, 256), F32)
        ext = jnp.zeros((rows, 256), F32)
        for h in range(heads):
            own = lanes(256, head_row(h, heads, False))
            s = dot(q * (own + at_mask).astype(BF), k, NT)
            m = jnp.max(s, axis=1, keepdims=True)
            e = jnp.exp(s - m)
            total = jnp.sum(e, axis=1, keepdims=True)
            a = (e * (1.0 / total)).astype(BF)
            out = out + dot(a, v * own.astype(BF))
            for i, part in enumerate(split3(-(m + jnp.log(total)))):
                ext = ext + part * lanes(256, lambda l: l == hw + 1 + 3 * h + i)
        p_ref[0, sl, 0:256] = (q.astype(F32) + ext).astype(BF)
        o_ref[0, sl] = out.astype(BF)

    @pl.when(b < long0)
    def _():
        for i in range(sub):
            pair(i * short_slot, short_slot, len_ref[b * sub + i])

    @pl.when(b >= long0)
    def _():
        pair(0, blk, len_ref[nshort + b - long0])


def attn_fwd(slot, lens, place, xs, xl, w, bias, prev, nshort, short_slot, heads, blk, slots):
    rows, d = xs.shape[0] + xl.shape[0], xs.shape[1]
    in_specs = blocks(blk, d, xs.shape[0] // blk) + [pl.BlockSpec((1, 768), lambda b, *_: (0, 0))]
    args = [xs, xl, bias]
    scratch = [pltpu.VMEM((768, d), BF), pltpu.VMEM((blk, d), BF)]
    aliases = {}
    if slot:
        in_specs += [pl.BlockSpec(memory_space=pl.ANY)] * 10
        args += list(w) + list(prev)
        aliases = {13: 0, 14: 1}
        r = w[0].shape[1]
        scratch += [pltpu.VMEM((8, r, d), F32), pltpu.SemaphoreType.DMA((8,))]
    else:
        in_specs.append(pl.BlockSpec(w.shape, lambda b, *_: (0, 0)))
        args.append(w)
    return pl.pallas_call(
        lambda *r: attn_fwd_kernel(
            *r, slot=slot, nshort=nshort, short_slot=short_slot, heads=heads, blk=blk
        ),
        grid_spec=pltpu.PrefetchScalarGridSpec(
            num_scalar_prefetch=2,
            grid=(rows // blk,),
            in_specs=in_specs,
            out_specs=[
                pl.BlockSpec((1, blk, 768), lambda b, *_: (slot, b, 0)),
                pl.BlockSpec((1, blk, 256), lambda b, *_: (slot, b, 0)),
            ],
            scratch_shapes=scratch,
        ),
        out_shape=[
            jax.ShapeDtypeStruct((slots, rows, 768), BF),
            jax.ShapeDtypeStruct((slots, rows, 256), BF),
        ],
        input_output_aliases=aliases,
        compiler_params=pltpu.CompilerParams(vmem_limit_bytes=60 * 2**20),
        cost_estimate=pl.CostEstimate(flops=14 * 10**9, bytes_accessed=2**23, transcendentals=0),
        name="attn_fwd",
    )(lens, place, *args)


def attn_bwd_pair(refs, sl, rows, heads):
    p_ref, o_ref, do_ref = refs
    hw = heads * HD
    q, k, v = p_ref[0, sl, 0:256], p_ref[0, sl, 256:512], p_ref[0, sl, 512:768]
    do = do_ref[0, sl]
    do32 = do.astype(F32)
    prod = do32 * o_ref[0, sl].astype(F32)
    ext = do32
    for h in range(heads):
        own = lanes(256, head_row(h, heads, False))
        delta = jnp.sum(prod * own, axis=1, keepdims=True)
        for i, part in enumerate(split3(-delta)):
            ext = ext + part * lanes(256, lambda l: l == hw + 1 + 3 * h + i)
    do_ext = ext.astype(BF)
    kt = k.T
    at_mask = lanes(256, lambda l: l == hw)
    dk = jnp.zeros((rows, 256), F32)
    dv = jnp.zeros((rows, 256), F32)
    dqs = []
    for h in range(heads):
        row = lanes(256, head_row(h, heads, True))
        qh = q * (row + at_mask).astype(BF)
        doh = do_ext * row.astype(BF)
        p = jnp.exp(dot(k, qh, NT))
        ds = (p * dot(v, doh, NT)).astype(BF)
        dv = dv + dot(p.astype(BF), doh)
        dk = dk + dot(ds, qh)
        dqs.append(dot(kt[h * HD : (h + 1) * HD], ds))
    dqs.append(jnp.zeros((256 - hw, rows), F32))
    dq = jnp.concatenate(dqs, 0).T * 0.125
    real = lanes(256, lambda l: l < hw)
    return dq.astype(BF), (dk * real).astype(BF), (dv * real).astype(BF)


def over_pairs(b, refs, dst, *, nshort, short_slot, heads, blk):
    sub = blk // short_slot
    long0 = nshort // sub

    def one(row, rows):
        sl = pl.ds(row, rows)
        for c, val in enumerate(attn_bwd_pair(refs, sl, rows, heads)):
            dst(sl, c, val)

    @pl.when(b < long0)
    def _():
        for i in range(sub):
            one(i * short_slot, short_slot)

    @pl.when(b >= long0)
    def _():
        one(0, blk)


def bwd_own_kernel(xs_ref, xl_ref, p_ref, o_ref, do_ref, dp_ref, gw_ref, gb_ref, **kw):
    b = pl.program_id(0)
    long0 = kw["nshort"] * kw["short_slot"] // kw["blk"]

    def dst(sl, c, val):
        dp_ref[sl, 256 * c : 256 * (c + 1)] = val

    over_pairs(b, (p_ref, o_ref, do_ref), dst, **kw)

    @pl.when(b == 0)
    def _():
        gw_ref[...] = jnp.zeros_like(gw_ref)
        gb_ref[...] = jnp.zeros_like(gb_ref)

    @pl.when(b < long0)
    def _():
        gw_ref[...] += dot(xs_ref[...], dp_ref[...], TN)

    @pl.when(b >= long0)
    def _():
        gw_ref[...] += dot(xl_ref[...], dp_ref[...], TN)

    gb_ref[...] += jnp.sum(dp_ref[...].astype(F32).reshape(-1, 8, 768), axis=0)


def bwd_own(xs, xl, p, o, do, blk, **kw):
    rows, d = xs.shape[0] + xl.shape[0], xs.shape[1]
    return pl.pallas_call(
        lambda *r: bwd_own_kernel(*r, blk=blk, **kw),
        grid=(rows // blk,),
        in_specs=blocks(blk, d, xs.shape[0] // blk)
        + [
            pl.BlockSpec((1, blk, 768), lambda b: (0, b, 0)),
            pl.BlockSpec((1, blk, 256), lambda b: (0, b, 0)),
            pl.BlockSpec((1, blk, 256), lambda b: (0, b, 0)),
        ],
        out_specs=[
            pl.BlockSpec((blk, 768), lambda b: (b, 0)),
            pl.BlockSpec((d, 768), lambda b: (0, 0)),
            pl.BlockSpec((8, 768), lambda b: (0, 0)),
        ],
        out_shape=[
            jax.ShapeDtypeStruct((rows, 768), BF),
            jax.ShapeDtypeStruct((d, 768), F32),
            jax.ShapeDtypeStruct((8, 768), F32),
        ],
        compiler_params=pltpu.CompilerParams(vmem_limit_bytes=60 * 2**20),
        cost_estimate=pl.CostEstimate(flops=18 * 10**9, bytes_accessed=2**23, transcendentals=0),
        name="attn_bwd_own",
    )(xs, xl, p, o, do)


def bwd_rest_kernel(
    place_ref, p_ref, o_ref, do_ref, own_ref, dh_ref, w_hbm, *refs, lo, **kw
):
    pieces, gs_ref, (gl_ref, dp_s, w_s, stage, sems, sem) = refs[:8], refs[8], refs[-6:]
    b, g = pl.program_id(0) + lo, pl.program_id(1)
    slots = w_s.shape[0]
    hw = kw["heads"] * HD
    long0 = kw["nshort"] * kw["short_slot"] // kw["blk"]

    @pl.when((b == lo) & (g == 0))
    def _():
        own = [
            pltpu.make_async_copy(
                w_hbm.at[pl.ds(c * hw, hw)], w_s.at[0, pl.ds(256 * c, hw)], sem.at[c]
            )
            for c in range(3)
        ]
        w_s[...] = jnp.zeros_like(w_s)
        for c in own:
            c.start()

        def store(n):
            def put(at):
                row = place_ref[1, n]

                @pl.when(row >= 0)
                def _():
                    @pl.loop(0, slots - 1)
                    def _(j):
                        w_s[j + 1, pl.ds(pl.multiple_of(row, 32), stage.shape[2])] = stage[
                            at, j
                        ].astype(BF)

            return put

        fetch([(pieces[n], None, store(n)) for n in range(8)], stage, sems, 3)
        for c in own:
            c.wait()

    @pl.when(g == 0)
    def _():
        dp_s[0] = own_ref[...]

    def dst(sl, c, val):
        dp_s[g + 1, sl, 256 * c : 256 * (c + 1)] = val

    over_pairs(b, (p_ref, o_ref, do_ref), dst, **kw)

    @pl.when(g == slots - 2)
    def _():
        acc = dh_ref[...]
        for j in range(slots):
            acc = acc + dot(dp_s[j], w_s[j])

        if lo < long0:

            @pl.when(b < long0)
            def _():
                gs_ref[...] = acc

        @pl.when(b >= long0)
        def _():
            gl_ref[...] = acc


def bwd_rest(lo, hi, prev, place, p, o, do, own_dp, dh, w_own, pieces, srows, blk, **kw):
    slots, rows, _ = p.shape
    d = dh.shape[1]
    r = pieces[0].shape[1]

    long0 = srows // blk
    assert lo == 0 or lo >= long0
    last = lo > 0

    def grp_map(b, g, *_):
        return (g + 1, b + lo, 0)

    return pl.pallas_call(
        lambda *r: bwd_rest_kernel(*r, lo=lo, blk=blk, **kw),
        grid_spec=pltpu.PrefetchScalarGridSpec(
            num_scalar_prefetch=1,
            grid=(hi - lo, slots - 1),
            in_specs=[
                pl.BlockSpec((1, blk, 768), grp_map),
                pl.BlockSpec((1, blk, 256), grp_map),
                pl.BlockSpec((1, blk, 256), grp_map),
                pl.BlockSpec((blk, 768), lambda b, g, *_: (b + lo, 0)),
                pl.BlockSpec((blk, d), lambda b, g, *_: (b + lo, 0)),
            ]
            + [pl.BlockSpec(memory_space=pl.ANY)] * (9 + last),
            out_specs=[pl.BlockSpec((blk, d), lambda b, g, *_: (b + lo - long0, 0))]
            if last
            else blocks(blk, d, long0),
            scratch_shapes=[
                pltpu.VMEM((slots, blk, 768), BF),
                pltpu.VMEM((slots, 768, d), BF),
                pltpu.VMEM((3, slots - 1, r, d), F32),
                pltpu.SemaphoreType.DMA((3,)),
                pltpu.SemaphoreType.DMA((3,)),
            ],
        ),
        out_shape=[
            jax.ShapeDtypeStruct((srows, d), F32),
            jax.ShapeDtypeStruct((rows - srows, d), F32),
        ][last:],
        input_output_aliases={15: 0} if last else {},
        compiler_params=pltpu.CompilerParams(vmem_limit_bytes=60 * 2**20),
        cost_estimate=pl.CostEstimate(flops=25 * 10**9, bytes_accessed=2**23, transcendentals=0),
        name="attn_bwd_rest",
    )(place, p, o, do, own_dp, dh, w_own, *pieces, *([prev] if last else []))


def norm_stats(h):
    center = h - jnp.mean(h, -1, keepdims=True)
    rstd = lax.rsqrt(jnp.mean(center * center, -1, keepdims=True) + EPS)
    return center * rstd, rstd


def norm_back(dy, xhat, rstd, gain):
    s = dy * gain
    return rstd * (
        s - jnp.mean(s, -1, keepdims=True) - xhat * jnp.mean(s * xhat, -1, keepdims=True)
    )


def gelu_both(u):
    phi = 0.5 + 0.5 * lax.erf(u * 0.7071067811865476)
    pdf = jnp.exp2(u * u * (-0.5 * 1.4426950408889634)) * 0.3989422804014327
    return u * phi, phi + u * pdf


def row8(x):
    return jnp.sum(x.reshape(-1, 8, x.shape[-1]), axis=0)


def ffn_kernel(place_ref, *refs, long0, hw):
    (xs_ref, xl_ref, cs_ref, cl_ref, o_ref, vec_ref, bup_ref, w1_hbm, wu_hbm, wd_hbm) = refs[:10]
    w1_pieces, w2_pieces = refs[10:18], refs[18:26]
    (es_ref, el_ref, dh_ref, do_ref, gall_ref) = refs[26:31]
    (wo_s, wu_s, wd_s, stage, sems, sem, g_s, gp_s, du_s, sm_s, x_s, c_s) = refs[31:]
    i = pl.program_id(0)
    slots, d, fl = wu_s.shape
    r = stage.shape[2]

    @pl.when(i == 0)
    def _():
        wo_s[...] = jnp.zeros_like(wo_s)
        own = [
            pltpu.make_async_copy(wu_hbm, wu_s.at[0], sem.at[0]),
            pltpu.make_async_copy(wd_hbm, wd_s.at[0], sem.at[1]),
            pltpu.make_async_copy(
                w1_hbm.at[pl.ds(3 * hw, hw)], wo_s.at[0, pl.ds(0, hw)], sem.at[2]
            ),
        ]
        for c in own:
            c.start()

        def store(dst, n):
            def put(at):
                row = pl.multiple_of(place_ref[0, n], 32)

                @pl.loop(0, slots - 1)
                def _(j):
                    dst[j + 1, pl.ds(row, r)] = stage[at, j].astype(BF)

            return put

        def store_out(n):
            def put(at):
                row = place_ref[2, n]

                @pl.when(row >= 0)
                def _():
                    @pl.loop(0, slots - 1)
                    def _(j):
                        wo_s[j + 1, pl.ds(pl.multiple_of(row, 32), r)] = stage[at, j].astype(BF)

            return put

        jobs = [(w1_pieces[n], None, store_out(n)) for n in range(8)]
        for n in range(8):
            jobs.append((w2_pieces[n].at[:, pl.ds(0, r)], None, store(wu_s, n)))
            jobs.append((w2_pieces[n].at[:, pl.ds(r, r)], None, store(wd_s, n)))
        fetch(jobs, stage, sems, 4)
        gall_ref[...] = jnp.zeros_like(gall_ref)
        sm_s[...] = jnp.zeros_like(sm_s)
        for c in own:
            c.wait()

    @pl.when(i < long0)
    def _():
        x_s[...] = xs_ref[...]
        c_s[...] = cs_ref[...]

    @pl.when(i >= long0)
    def _():
        x_s[...] = xl_ref[...]
        c_s[...] = cl_ref[...]

    def vec(n):
        return vec_ref[n : n + 1].astype(F32)

    attn = dot(o_ref[0], wo_s[0])
    for j in range(1, slots):
        attn = attn + dot(o_ref[j], wo_s[j])
    xhat1, rstd1 = norm_stats(x_s[...].astype(F32) + attn + vec(0))
    y1 = xhat1 * vec(2) + vec(4)
    y1b = y1.astype(BF)
    ffn = jnp.zeros_like(y1)
    for j in range(slots):
        u = dot(y1b, wu_s[j]) + bup_ref[j : j + 1]
        g, gp = gelu_both(u)
        gb = g.astype(BF)
        g_s[j] = gb
        gp_s[j] = gp
        ffn = ffn + dot(gb, wd_s[j])
    xhat2, rstd2 = norm_stats(y1 + ffn + vec(1))
    enc = (xhat2 * vec(3) + vec(5)).astype(BF)

    @pl.when(i < long0)
    def _():
        es_ref[...] = enc

    @pl.when(i >= long0)
    def _():
        el_ref[...] = enc

    dy = c_s[...].astype(F32)
    dh2 = norm_back(dy, xhat2, rstd2, vec(3))
    dz = dh2.astype(BF)
    sm_s[1] += row8(dh2)
    sm_s[3] += row8(dy * xhat2)
    sm_s[5] += row8(dy)
    dy1 = dh2
    for j in range(slots):
        du = (dot(dz, wd_s[j], NT) * gp_s[j]).astype(BF)
        du_s[j] = du
        dy1 = dy1 + dot(du, wu_s[j], NT)
    gall_ref[:, 0:fl] += dot(y1b, du_s[0], TN)
    gall_ref[:, fl : 2 * fl] += dot(dz, g_s[0], TN)
    sm_s[6] += row8(du_s[0].astype(F32))
    dh1 = norm_back(dy1, xhat1, rstd1, vec(2))
    dh_ref[...] = dh1
    da = dh1.astype(BF)
    sm_s[0] += row8(dh1)
    sm_s[2] += row8(dy1 * xhat1)
    sm_s[4] += row8(dy1)
    gall_ref[:, 2 * fl : 2 * fl + 256] += dot(da, o_ref[0], TN)
    for j in range(slots):
        do_ref[j] = dot(da, wo_s[j], NT).astype(BF)

    @pl.when(i == pl.num_programs(0) - 1)
    def _():
        small = jnp.sum(sm_s[...], axis=1)
        small = jnp.concatenate([small, jnp.zeros((120, d), F32)], 0)
        gall_ref[:, 2 * fl + 256 :] = small.T


def ffn_block(place, xs, xl, cs, cl, o, vecs, bup, own, pieces, hw, blk):
    srows, d = xs.shape
    rows = srows + xl.shape[0]
    slots = o.shape[0]
    fl = own[1].shape[1]
    r = pieces[0].shape[1]
    long0 = srows // blk
    row = lambda i, *_: (i, 0)
    grp = lambda i, *_: (0, i, 0)
    const = lambda i, *_: (0, 0)
    return pl.pallas_call(
        lambda *r: ffn_kernel(*r, long0=long0, hw=hw),
        grid_spec=pltpu.PrefetchScalarGridSpec(
            num_scalar_prefetch=1,
            grid=(rows // blk,),
            in_specs=blocks(blk, d, long0)
            + blocks(blk, d, long0)
            + [
                pl.BlockSpec((slots, blk, 256), grp),
                pl.BlockSpec((8, d), const),
                pl.BlockSpec((slots, fl), const),
            ]
            + [pl.BlockSpec(memory_space=pl.ANY)] * 19,
            out_specs=blocks(blk, d, long0)
            + [
                pl.BlockSpec((blk, d), row),
                pl.BlockSpec((slots, blk, 256), grp),
                pl.BlockSpec((d, 2 * fl + 384), const, pipeline_mode=pl.Buffered(1)),
            ],
            scratch_shapes=[
                pltpu.VMEM((slots, 256, d), BF),
                pltpu.VMEM((slots, d, fl), BF),
                pltpu.VMEM((slots, fl, d), BF),
                pltpu.VMEM((4, slots - 1, r, d), F32),
                pltpu.SemaphoreType.DMA((4,)),
                pltpu.SemaphoreType.DMA((3,)),
                pltpu.VMEM((slots, blk, fl), BF),
                pltpu.VMEM((slots, blk, fl), F32),
                pltpu.VMEM((slots, blk, fl), BF),
                pltpu.VMEM((8, 8, d), F32),
                pltpu.VMEM((blk, d), BF),
                pltpu.VMEM((blk, d), BF),
            ],
        ),
        out_shape=[
            jax.ShapeDtypeStruct((srows, d), BF),
            jax.ShapeDtypeStruct((rows - srows, d), BF),
            jax.ShapeDtypeStruct((rows, d), F32),
            jax.ShapeDtypeStruct((slots, rows, 256), BF),
            jax.ShapeDtypeStruct((d, 2 * fl + 384), F32),
        ],
        compiler_params=pltpu.CompilerParams(vmem_limit_bytes=62 * 2**20),
        cost_estimate=pl.CostEstimate(flops=80 * 10**9, bytes_accessed=2**25, transcendentals=0),
        name="ffn_block",
    )(place, xs, xl, cs, cl, o, vecs, bup, *own, *pieces)


class Wires:
    def __init__(self, n_dp, n_tensor):
        self.n_dp, self.n_tensor = n_dp, n_tensor
        self.first = [(i, i ^ (4 if i & 1 else 2)) for i in range(n_dp)]
        self.second = [(i, i ^ (2 if i & 1 else 4)) for i in range(n_dp)]
        self.pair = [(i, i ^ 1) for i in range(n_dp)]
        me = lax.axis_index("dp")
        odd = (me & 1).astype(jnp.int32)
        a, b = 2 + 2 * odd, 4 - 2 * odd
        masks = [0, a, b, 6, 1, 1 ^ b, 1 ^ a, 7]
        self.low = (me & 7).astype(jnp.int32)
        self.odd, self.x, self.y = odd, (self.low >> 1) & 1, self.low >> 2
        self.source = jnp.stack([jnp.asarray(self.low ^ m, jnp.int32) for m in masks])

    def piece(self, shard):
        extra = self.n_dp // 8
        r = shard.shape[0] // self.n_dp
        at = (self.low * extra + lax.axis_index("dp") // 8) * r
        return lax.dynamic_slice_in_dim(shard, at, r, 0).astype(F32)

    def along_tensor(self, piece):
        n = self.n_tensor
        return [
            lax.ppermute(piece, "tensor", [(i, (i + s) % n) for i in range(n)]) for s in range(1, n)
        ]

    def whole_eighth(self, z):
        if self.n_dp == 8:
            return z
        groups = [[g + 8 * e for e in range(self.n_dp // 8)] for g in range(8)]
        return lax.all_gather(z, "dp", axis=z.ndim - 2, tiled=True, axis_index_groups=groups)

    def first_hop(self, z):
        return lax.ppermute(z, "dp", self.first), lax.ppermute(z, "dp", self.second)

    def second_hop(self, a):
        return lax.ppermute(a, "dp", self.second)

    def to_pair(self, x):
        return lax.ppermute(x, "dp", self.pair)


    def split(self, g):
        rows, width = g.shape
        return g.reshape(self.n_dp // 8, 4, 2, rows // self.n_dp, width)

    def halve_pair(self, g):
        return self.to_pair(lax.dynamic_index_in_dim(g, 1 - self.odd, 2, keepdims=False))

    def sum_pair(self, g, got):
        return lax.dynamic_index_in_dim(g, self.odd, 2, keepdims=False) + got

    def two(self, h, x, y):
        n = jnp.where(self.odd == 1, 2 * y, x)
        m = jnp.where(self.odd == 1, 2 * y + 1, x + 2)
        return jnp.concatenate([lax.dynamic_slice_in_dim(h, i, 1, 1) for i in (n, m)], 1)

    def halve_first(self, h):
        return lax.ppermute(self.two(h, 1 - self.x, 1 - self.y), "dp", self.first)

    def sum_first(self, h, got):
        return self.two(h, self.x, self.y) + got

    def halve_second(self, k):
        at = jnp.where(self.odd == 1, self.x, self.y)
        return lax.ppermute(lax.dynamic_index_in_dim(k, 1 - at, 1, keepdims=False), "dp", self.second)

    def sum_second(self, k, got):
        at = jnp.where(self.odd == 1, self.x, self.y)
        out = lax.dynamic_index_in_dim(k, at, 1, keepdims=False) + got
        if self.n_dp == 8:
            return out[0]
        groups = [[g + 8 * e for e in range(self.n_dp // 8)] for g in range(8)]
        return lax.psum_scatter(out, "dp", scatter_dimension=0, axis_index_groups=groups)


def after(x, *others):
    return lax.optimization_barrier((x, *others))[0]


def make(n_dp, n_tensor):
    def on_device(
        short_tokens,
        short_lengths,
        long_tokens,
        long_lengths,
        w_qkv,
        b_qv,
        w_out,
        res_biases,
        ln_gains,
        ln_shifts,
        w_up,
        b_up,
        w_down,
        short_cotangent,
        long_cotangent,
    ):
        ns, ss, d = short_tokens.shape
        nl, ls, _ = long_tokens.shape
        srows = ns * ss
        heads, hd = b_qv.shape[1], b_qv.shape[2]
        hw = heads * hd
        blk = ls
        kw = dict(nshort=ns, short_slot=ss, heads=heads, blk=blk)
        wires = Wires(n_dp, n_tensor)
        r = w_up.shape[0] // 8

        w1_own = jnp.concatenate([w_qkv.transpose(0, 2, 1).reshape(3 * hw, d), w_out], 0)
        tail = jnp.zeros((d - 2 * hw,), F32)
        small = jnp.stack([b_up[0].astype(F32), jnp.concatenate([b_qv.reshape(2 * hw).astype(F32), tail])])
        small = jnp.concatenate([small, jnp.zeros((6, d), F32)], 0)
        piece = wires.piece(w1_own)
        pr = piece.shape[0]
        z = wires.along_tensor(jnp.concatenate([small, piece], 0))
        row = wires.source * r
        c = row // hw
        place = jnp.stack(
            [row, jnp.where(c < 3, c * 256 + row - c * hw, -1), jnp.where(c < 3, -1, row - 3 * hw)]
        )

        one = np.zeros((256 - hw,), np.float32)
        one[1 : 1 + 3 * heads] = 1.0
        one = jnp.asarray(one)

        def bias_of(sm):
            zero = jnp.zeros((256 - hw,), F32)
            none = jnp.zeros((hw,), F32)
            return jnp.concatenate([sm[1, :hw], zero, none, one, sm[1, hw : 2 * hw], one])[None]

        xs, xl = short_tokens.reshape(srows, d), long_tokens.reshape(-1, d)
        cs, cl = short_cotangent.reshape(srows, d), long_cotangent.reshape(-1, d)
        lens = jnp.concatenate([short_lengths, long_lengths])
        po = attn_fwd(0, lens, place, xs, xl, w1_own, bias_of(small), None, slots=n_tensor, **kw)

        t1 = wires.whole_eighth(after(jnp.stack([x[8:] for x in z]), po[1]))
        a1, b1 = wires.first_hop(t1)
        piece2 = after(jnp.stack([wires.piece(w_up), wires.piece(w_down)]), po[1])
        z2 = wires.along_tensor(piece2)
        c1 = wires.second_hop(after(a1, z2[0]))
        w1 = [t1, a1, b1, c1]
        w1 += [wires.to_pair(x) for x in w1[:3]] + [wires.to_pair(after(c1, z2[2]))]
        for s in range(1, n_tensor):
            po = attn_fwd(s, lens, place, xs, xl, w1, bias_of(z[s - 1]), po, slots=n_tensor, **kw)
            if s == 1:
                *z2, p, o = lax.optimization_barrier((*z2, *po))
                po = p, o
                t2 = wires.whole_eighth(jnp.stack(z2))
                t2 = t2.reshape(n_tensor - 1, -1, d)
                a2, b2 = wires.first_hop(t2)
        t2, a2, b2, *po = lax.optimization_barrier((t2, a2, b2, *po))
        w2 = [t2, a2, b2, wires.second_hop(a2)]
        w2 += [wires.to_pair(x) for x in w2]
        p, o = po
        bup = jnp.stack([x[0] for x in [small] + z])
        vecs = jnp.concatenate([res_biases, ln_gains, ln_shifts, jnp.zeros((2, d), BF)], 0).astype(F32)
        es, el, dh, do, gall = ffn_block(
            place, xs, xl, cs, cl, o, vecs, bup, [w1_own, w_up, w_down], w1 + w2, hw, 256
        )
        fl = w_up.shape[1]
        gall = wires.split(gall)
        got = wires.halve_pair(gall)
        dp_own, gw, gb = bwd_own(xs, xl, p, o, do, **kw)
        gall = wires.sum_pair(gall, after(got, dp_own))
        got = wires.halve_first(gall)
        gb = gb.sum(0).reshape(3, 256)
        gb = jnp.stack([gb[0, :hw], gb[2, :hw]]).reshape(2 * heads, n_dp, hd // n_dp)
        gb = gb.transpose(1, 0, 2).reshape(n_dp, 1, -1)
        gw = lax.dynamic_update_slice(gw.reshape(n_dp, d // n_dp, 768), gb, (0, 0, hw))
        gw = wires.split(gw.reshape(d, 768))
        gotw = wires.halve_pair(gw)
        nb = (ns * ss + nl * ls) // blk
        rest = (place, p, o, do, dp_own, dh, w1_own, w1, srows)
        gs, gl = bwd_rest(0, nb // 2, None, *rest, **kw)
        got, gotw, gl = lax.optimization_barrier((got, gotw, gl))
        gall = wires.sum_first(gall, got)
        got = wires.halve_second(gall)
        gw = wires.sum_pair(gw, gotw)
        gotw = wires.halve_first(gw)
        (gl,) = bwd_rest(nb // 2, nb, gl, *rest, **kw)
        got, gotw, gl = lax.optimization_barrier((got, gotw, gl))
        gw = wires.sum_first(gw, gotw)
        gotw = wires.halve_second(gw)
        gall = wires.sum_second(gall, got)
        gw = wires.sum_second(gw, gotw)
        small_shard = gall[:, 2 * fl + 256 : 2 * fl + 264].T
        gqkv = gw.reshape(-1, 3, 256)[:, :, :hw].transpose(1, 0, 2)
        qv_shard = gw[0, hw : hw + 2 * hw // n_dp].reshape(2, heads, hd // n_dp)
        return (
            es.reshape(ns, ss, d),
            el.reshape(nl, ls, d),
            gs.reshape(ns, ss, d),
            gl.reshape(nl, ls, d),
            gqkv,
            qv_shard,
            gall[:, 2 * fl : 2 * fl + hw].T,
            small_shard[0:2],
            small_shard[2:4],
            small_shard[4:6],
            gall[:, :fl],
            small_shard[6:7],
            gall[:, fl : 2 * fl].T,
        )

    return on_device


def solution(mesh):
    tok = P("dp", None, None)
    return jax.shard_map(
        make(mesh.shape["dp"], mesh.shape["tensor"]),
        mesh=mesh,
        in_specs=(
            tok,
            P("dp"),
            tok,
            P("dp"),
            P(None, None, "tensor"),
            P(None, "tensor", None),
            P("tensor", None),
            P(),
            P(),
            P(),
            P(None, "tensor"),
            P("tensor", None),
            P("tensor", None),
            tok,
            tok,
        ),
        out_specs=(
            tok,
            tok,
            tok,
            tok,
            P(None, "dp", "tensor"),
            P(None, "tensor", "dp"),
            P("tensor", "dp"),
            P(None, "dp"),
            P(None, "dp"),
            P(None, "dp"),
            P("dp", "tensor"),
            P("tensor", "dp"),
            P("tensor", "dp"),
        ),
        check_vma=False,
    )
```

profile of v0, /device:TPU:0, one launch (start us, length us, event | category | flops | bytes accessed | tf_op | source)
XLA Modules:
  0.0 367.9 jit_solution(9605066013650064195)
XLA Ops:
  2.3 1.0 fusion.2
  3.5 5.1 %collective-permute-start.5 = (f32[104,768]{1,0:T(8,128)S(1)}, f32[104,768]{1,0:T(8,128)S(1)}, u32[]{:S(2)}, u32[]{:S(2)}) collective-permute-start(f32[104,768]{1,0:T(8,128)S(1)} %pad_maximum_fusion.5), channel_id=1, source_target_pairs={{0,3},{1,0},{2,1},{3,2},{4,7},{5,4},{6,5},{7,6},{8,11},{9,8},{10,9... | collective-permute-start | bytes 958472 | tf_op jit(solution)/shard_map/ppermute | solution.py:630
  8.6 1.0 collective-permute-start.3
  9.7 1.1 pad_maximum_fusion.1.r_5_.r_8_.r_6_
  12.8 15.5 %attn_fwd.4 = (bf16[4,2048,768]{2,1,0:T(8,128)(2,1)}, bf16[4,2048,256]{2,1,0:T(8,128)(2,1)}) custom-call(s32[5]{0:T(128)} %pad_add_fusion.1.r_0_, s32[3,8]{1,0:T(4,128)} %pad_add_fusion.r_1_.r_0_, bf16[512,768]{1,0:T(8,128)(2,1)} %bitcast.103, bf16[1536,768]{1,0:T(8,128)(2,1)} %bitcast.96, f32[1,768]{1,0:T(1,128)} %broadcast_in_dim.23.r_4_, ...), custom_call_target="tpu_custom_call" | custom-call | flops 14000000000 | bytes 8388608 | tf_op jit(solution)/shard_map/attn_fwd/pallas_call | solution.py:162
  28.3 7.5 %collective-permute-done.4 = f32[104,768]{1,0:T(8,128)S(1)} collective-permute-done((f32[104,768]{1,0:T(8,128)S(1)}, f32[104,768]{1,0:T(8,128)S(1)}, u32[]{:S(2)}, u32[]{:S(2)}) %collective-permute-start.4) | collective-permute-done | bytes 319520 | tf_op jit(solution)/shard_map/ppermute | solution.py:630
  36.0 1.6 collective-permute-start.6
  37.5 1.0 dynamic-slice_bitcast_fusion.4
  38.6 0.9 collective-permute-start
  39.5 1.5 collective-permute-start.7
  41.0 13.4 %collective-permute-done = f32[2,96,768]{2,1,0:T(8,128)S(1)} collective-permute-done((f32[2,96,768]{2,1,0:T(8,128)S(1)}, f32[2,96,768]{2,1,0:T(8,128)S(1)}, u32[]{:S(2)}, u32[]{:S(2)}) %collective-permute-start) | collective-permute-done | bytes 589856 | tf_op jit(solution)/shard_map/ppermute | solution.py:630
  54.4 3.0 collective-permute-done.6.r_6_.r_12_.r_8_
  57.4 2.5 collective-permute-start.8
  61.1 9.2 %collective-permute-done.2 = f32[2,96,768]{2,1,0:T(8,128)S(1)} collective-permute-done((f32[2,96,768]{2,1,0:T(8,128)S(1)}, f32[2,96,768]{2,1,0:T(8,128)S(1)}, u32[]{:S(2)}, u32[]{:S(2)}) %collective-permute-start.2) | collective-permute-done | bytes 589856 | tf_op jit(solution)/shard_map/ppermute | solution.py:630
  70.4 0.9 collective-permute-done.8.r_8_.r_14_.r_10_
  71.3 3.0 collective-permute-start.1
  74.3 0.8 fusion.4
  75.8 0.8 fusion.3
  77.3 0.8 fusion.5
  78.8 16.7 %attn_fwd.5 = (bf16[4,2048,768]{2,1,0:T(8,128)(2,1)}, bf16[4,2048,256]{2,1,0:T(8,128)(2,1)}) custom-call(s32[5]{0:T(128)} %pad_add_fusion.1.r_0_, s32[3,8]{1,0:T(4,128)} %pad_add_fusion.r_1_.r_0_, bf16[512,768]{1,0:T(8,128)(2,1)} %bitcast.104, bf16[1536,768]{1,0:T(8,128)(2,1)} %bitcast.97, ...), custom_call_target="tpu_custom_call", output_to_operand_aliasing={{0}: (13, {}), {1}: (14, {})} | custom-call | flops 14000000000 | bytes 8388608 | tf_op jit(solution)/shard_map/attn_fwd/pallas_call | solution.py:162
  95.6 5.3 %collective-permute-done.1 = f32[2,96,768]{2,1,0:T(8,128)S(1)} collective-permute-done((f32[2,96,768]{2,1,0:T(8,128)S(1)}, f32[2,96,768]{2,1,0:T(8,128)S(1)}, u32[]{:S(2)}, u32[]{:S(2)}) %collective-permute-start.1) | collective-permute-done | bytes 589856 | tf_op jit(solution)/shard_map/ppermute | solution.py:630
  100.9 0.8 copy-done.6
  101.7 1.4 pad_maximum_fusion.r_19_
  103.1 1.6 collective-permute-start.14
  105.0 16.7 %attn_fwd.6 = (bf16[4,2048,768]{2,1,0:T(8,128)(2,1)}, bf16[4,2048,256]{2,1,0:T(8,128)(2,1)}) custom-call(s32[5]{0:T(128)} %pad_add_fusion.1.r_0_, s32[3,8]{1,0:T(4,128)} %pad_add_fusion.r_1_.r_0_, bf16[512,768]{1,0:T(8,128)(2,1)} %bitcast.105, bf16[1536,768]{1,0:T(8,128)(2,1)} %bitcast.98, ...), custom_call_target="tpu_custom_call", output_to_operand_aliasing={{0}: (13, {}), {1}: (14, {})} | custom-call | flops 14000000000 | bytes 8388608 | tf_op jit(solution)/shard_map/attn_fwd/pallas_call | solution.py:162
  121.8 16.9 %attn_fwd.7 = (bf16[4,2048,768]{2,1,0:T(8,128)(2,1)}, bf16[4,2048,256]{2,1,0:T(8,128)(2,1)}) custom-call(s32[5]{0:T(128)} %pad_add_fusion.1.r_0_, s32[3,8]{1,0:T(4,128)} %pad_add_fusion.r_1_.r_0_, bf16[512,768]{1,0:T(8,128)(2,1)} %bitcast.106, bf16[1536,768]{1,0:T(8,128)(2,1)} %bitcast.99, ...), custom_call_target="tpu_custom_call", output_to_operand_aliasing={{0}: (13, {}), {1}: (14, {})} | custom-call | flops 14000000000 | bytes 8388608 | tf_op jit(solution)/shard_map/attn_fwd/pallas_call | solution.py:162
  138.7 6.1 %collective-permute-done.14.r_21_ = f32[3,192,768]{2,1,0:T(8,128)} collective-permute-done((f32[3,192,768]{2,1,0:T(8,128)S(1)}, f32[3,192,768]{2,1,0:T(8,128)}, u32[]{:S(2)}, u32[]{:S(2)}) %collective-permute-start.14) | collective-permute-done | bytes 1769504 | tf_op jit(solution)/shard_map/ppermute | solution.py:640
  146.0 21.6 %collective-permute-done.15.r_22_ = f32[3,192,768]{2,1,0:T(8,128)} collective-permute-done((f32[3,192,768]{2,1,0:T(8,128)}, f32[3,192,768]{2,1,0:T(8,128)}, u32[]{:S(2)}, u32[]{:S(2)}) %collective-permute-start.15) | collective-permute-done | bytes 1769504 | tf_op jit(solution)/shard_map/ppermute | solution.py:643
  169.0 2.6 collective-permute-done.19.r_26_
  171.6 85.3 %ffn_block.1 = (bf16[512,768]{1,0:T(8,128)(2,1)}, bf16[1536,768]{1,0:T(8,128)(2,1)}, f32[2048,768]{1,0:T(8,128)}, bf16[4,2048,256]{2,1,0:T(8,128)(2,1)}, f32[768,1920]{1,0:T(8,128)}) custom-call(s32[3,8]{1,0:T(4,128)} %pad_add_fusion.r_1_.r_0_, bf16[512,768]{1,0:T(8,128)(2,1)} %bitcast.107, bf16[1536,768]{1,0:T(8,128)(2,1)} %bitcast.100, ...), custom_call_target="tpu_custom_call" | custom-call | flops 80000000000 | bytes 33554432 | tf_op jit(solution)/shard_map/ffn_block/pallas_call | solution.py:560
  257.0 3.6 dynamic-slice_bitcast_fusion
  260.8 18.4 %attn_bwd_own.1 = (bf16[2048,768]{1,0:T(8,128)(2,1)}, f32[768,768]{1,0:T(8,128)}, f32[8,768]{1,0:T(8,128)}) custom-call(bf16[512,768]{1,0:T(8,128)(2,1)} %bitcast.108, bf16[1536,768]{1,0:T(8,128)(2,1)} %bitcast.101, bf16[4,2048,768]{2,1,0:T(8,128)(2,1)} %get-tuple-element.75.r_2_.r_1_, bf16[4,2048,256]{2,1,0:T(8,128)(2,1)} %get-tuple-element.69.r_5_.r_3_.r_2_, ...), custom_call_target="tpu_custom_call" | custom-call | flops 17999998976 | bytes 8388608 | tf_op jit(solution)/shard_map/attn_bwd_own/pallas_call | solution.py:267
  280.2 2.6 dynamic_update_slice.3
  282.8 2.4 dynamic-slice_bitcast_fusion.1
  285.5 2.1 bitcast_add_fusion
  287.8 1.3 pad_maximum_fusion.2
  289.1 0.8 collective-permute-start.21
  289.9 30.4 %attn_bwd_rest.2 = (f32[512,768]{1,0:T(8,128)}, f32[1536,768]{1,0:T(8,128)}) custom-call(s32[3,8]{1,0:T(4,128)} %pad_add_fusion.r_1_.r_0_, bf16[4,2048,768]{2,1,0:T(8,128)(2,1)} %get-tuple-element.75.r_2_.r_1_, bf16[4,2048,256]{2,1,0:T(8,128)(2,1)} %get-tuple-element.69.r_5_.r_3_.r_2_, bf16[4,2048,256]{2,1,0:T(8,128)(2,1)} %get-tuple-element.76.r_4_.r_3_, ...), custom_call_target="tpu_custom_call" | custom-call | flops 24999999488 | bytes 8388608 | tf_op jit(solution)/shard_map/attn_bwd_rest/pallas_call | solution.py:369
  320.4 1.4 bitcast_add_fusion.1
  321.9 0.9 pad_maximum_fusion.4
  322.8 1.3 collective-permute-start.24
  324.1 1.5 maximum_add_fusion
  325.7 0.8 collective-permute-start.23
  326.5 31.3 %attn_bwd_rest.3 = f32[1536,768]{1,0:T(8,128)} custom-call(s32[3,8]{1,0:T(4,128)} %pad_add_fusion.r_1_.r_0_, bf16[4,2048,768]{2,1,0:T(8,128)(2,1)} %get-tuple-element.75.r_2_.r_1_, bf16[4,2048,256]{2,1,0:T(8,128)(2,1)} %get-tuple-element.69.r_5_.r_3_.r_2_, bf16[4,2048,256]{2,1,0:T(8,128)(2,1)} %get-tuple-element.76.r_4_.r_3_, ...), custom_call_target="tpu_custom_call", output_to_operand_aliasing={{}: (15, {})} | custom-call | flops 24999999488 | bytes 8388608 | tf_op jit(solution)/shard_map/attn_bwd_rest/pallas_call | solution.py:369
  357.8 1.2 fusion
  359.1 1.4 collective-permute-start.25
  364.0 0.8 slice_bitcast_fusion.1
  364.8 1.1 collective-permute-done.25
  (128 shorter events, 17.3 us)
Async XLA Ops:
  0.6 9.0 %copy-start.3 = (bf16[192,768]{1,0:T(8,128)(2,1)S(1)}, bf16[192,768]{1,0:T(8,128)(2,1)}, u32[]{:S(2)}) copy-start(bf16[192,768]{1,0:T(8,128)(2,1)} %param.22) | copy-start | bytes 884740
  0.7 9.0 %copy-start = (bf16[3,768,192]{1,2,0:T(8,128)(2,1)S(1)}, bf16[3,768,192]{1,2,0:T(8,128)(2,1)}, u32[]{:S(2)}) copy-start(bf16[3,768,192]{1,2,0:T(8,128)(2,1)} %param.20) | copy-start | bytes 2654212
  3.3 7.6 %copy-start.10 = (f32[64]{0:T(128)S(1)}, f32[64]{0:T(128)}, u32[]{:S(2)}) copy-start(f32[64]{0:T(128)} %constant.94.clone) | copy-start | bytes 772
  3.3 8.3 %copy-start.14 = (s32[3]{0:T(128)S(1)}, s32[3]{0:T(128)}, u32[]{:S(2)}) copy-start(s32[3]{0:T(128)} %param.19) | copy-start | bytes 40
  3.3 8.3 %copy-start.15 = (s32[2]{0:T(128)S(1)}, s32[2]{0:T(128)}, u32[]{:S(2)}) copy-start(s32[2]{0:T(128)} %param.17) | copy-start | bytes 28
  3.5 24.8 %collective-permute-start.5 = (f32[104,768]{1,0:T(8,128)S(1)}, f32[104,768]{1,0:T(8,128)S(1)}, u32[]{:S(2)}, u32[]{:S(2)}) collective-permute-start(f32[104,768]{1,0:T(8,128)S(1)} %pad_maximum_fusion.5), channel_id=1, source_target_pairs={{0,3},{1,0},{2,1},{3,2},{4,7},{5,4},{6,5},{7,6},{8,11},{9,8},{10,9... | collective-permute-start | bytes 958472 | tf_op jit(solution)/shard_map/ppermute | solution.py:630
  8.6 27.2 %collective-permute-start.4 = (f32[104,768]{1,0:T(8,128)S(1)}, f32[104,768]{1,0:T(8,128)S(1)}, u32[]{:S(2)}, u32[]{:S(2)}) collective-permute-start(f32[104,768]{1,0:T(8,128)S(1)} %pad_maximum_fusion.5), channel_id=1, source_target_pairs={{0,2},{1,3},{2,0},{3,1},{4,6},{5,7},{6,4},{7,5},{8,10},{9,11},{10,... | collective-permute-start | bytes 958472 | tf_op jit(solution)/shard_map/ppermute | solution.py:630
  8.6 27.3 %collective-permute-start.3 = (f32[104,768]{1,0:T(8,128)S(1)}, f32[104,768]{1,0:T(8,128)S(1)}, u32[]{:S(2)}, u32[]{:S(2)}) collective-permute-start(f32[104,768]{1,0:T(8,128)S(1)} %pad_maximum_fusion.5), channel_id=1, source_target_pairs={{0,1},{1,2},{2,3},{3,0},{4,5},{5,6},{6,7},{7,4},{8,9},{9,10},{10,1... | collective-permute-start | bytes 958472 | tf_op jit(solution)/shard_map/ppermute | solution.py:630
  28.3 7.7 %copy-start.8 = (f32[104,768]{1,0:T(8,128)}, f32[104,768]{1,0:T(8,128)S(1)}, u32[]{:S(2)}) copy-start(f32[104,768]{1,0:T(8,128)S(1)} %collective-permute-done.5) | copy-start | bytes 958468
  35.8 2.7 copy-start.9
  35.8 2.8 copy-start.7
  36.0 42.9 %copy-start.4 = (f32[3,96,768]{2,1,0:T(8,128)}, f32[3,96,768]{2,1,0:T(8,128)S(1)}, u32[]{:S(2)}) copy-start(f32[3,96,768]{2,1,0:T(8,128)S(1)} %pad_maximum_fusion.3.r_5_.r_11_.r_7_) | copy-start | bytes 2654212
  36.0 21.4 %collective-permute-start.6 = (f32[3,96,768]{2,1,0:T(8,128)S(1)}, f32[3,96,768]{2,1,0:T(8,128)}, u32[]{:S(2)}, u32[]{:S(2)}) collective-permute-start(f32[3,96,768]{2,1,0:T(8,128)S(1)} %pad_maximum_fusion.3.r_5_.r_11_.r_7_), channel_id=1, source_target_pairs={{0,8},{4,20},{8,0},{12,28},{16,24},{20,4},{24,16},{28,12},{1,9},{5... | collective-permute-start | bytes 2654216 | tf_op jit(solution)/shard_map/ppermute | solution.py:640
  38.6 15.8 %collective-permute-start = (f32[2,96,768]{2,1,0:T(8,128)S(1)}, f32[2,96,768]{2,1,0:T(8,128)S(1)}, u32[]{:S(2)}, u32[]{:S(2)}) collective-permute-start(f32[2,96,768]{2,1,0:T(8,128)S(1)} %maximum_convert_fusion), channel_id=1, source_target_pairs={{0,1},{1,2},{2,3},{3,0},{4,5},{5,6},{6,7},{7,4},{8,9},{9,10},{10,1... | collective-permute-start | bytes 1769480 | tf_op jit(solution)/shard_map/ppermute | solution.py:630
  39.5 21.6 %collective-permute-start.7 = (f32[3,96,768]{2,1,0:T(8,128)S(1)}, f32[3,96,768]{2,1,0:T(8,128)}, u32[]{:S(2)}, u32[]{:S(2)}) collective-permute-start(f32[3,96,768]{2,1,0:T(8,128)S(1)} %pad_maximum_fusion.3.r_5_.r_11_.r_7_), channel_id=1, source_target_pairs={{0,16},{4,12},{8,24},{12,4},{16,0},{20,28},{24,8},{28,20},{1,17},{... | collective-permute-start | bytes 2654216 | tf_op jit(solution)/shard_map/ppermute | solution.py:640
  57.4 13.9 %collective-permute-start.8 = (f32[3,96,768]{2,1,0:T(8,128)}, f32[3,96,768]{2,1,0:T(8,128)}, u32[]{:S(2)}, u32[]{:S(2)}) collective-permute-start(f32[3,96,768]{2,1,0:T(8,128)} %collective-permute-done.6.r_6_.r_12_.r_8_), channel_id=1, source_target_pairs={{0,16},{4,12},{8,24},{12,4},{16,0},{20,28},{24,8},{28,20},{1,17},{... | collective-permute-start | bytes 2654216 | tf_op jit(solution)/shard_map/ppermute | solution.py:643
  60.0 10.4 %collective-permute-start.2 = (f32[2,96,768]{2,1,0:T(8,128)S(1)}, f32[2,96,768]{2,1,0:T(8,128)S(1)}, u32[]{:S(2)}, u32[]{:S(2)}) collective-permute-start(f32[2,96,768]{2,1,0:T(8,128)S(1)} %maximum_convert_fusion), channel_id=1, source_target_pairs={{0,3},{1,0},{2,1},{3,2},{4,7},{5,4},{6,5},{7,6},{8,11},{9,8},{10,9... | collective-permute-start | bytes 1769480 | tf_op jit(solution)/shard_map/ppermute | solution.py:630
  60.5 18.3 %collective-permute-start.9 = (f32[3,96,768]{2,1,0:T(8,128)S(1)}, f32[3,96,768]{2,1,0:T(8,128)}, u32[]{:S(2)}, u32[]{:S(2)}) collective-permute-start(f32[3,96,768]{2,1,0:T(8,128)S(1)} %pad_maximum_fusion.3.r_5_.r_11_.r_7_), channel_id=1, source_target_pairs={{0,4},{4,0},{8,12},{12,8},{16,20},{20,16},{24,28},{28,24},{1,5},{5... | collective-permute-start | bytes 2654216 | tf_op jit(solution)/shard_map/ppermute | solution.py:646
  60.6 18.3 %collective-permute-start.10 = (f32[3,96,768]{2,1,0:T(8,128)}, f32[3,96,768]{2,1,0:T(8,128)}, u32[]{:S(2)}, u32[]{:S(2)}) collective-permute-start(f32[3,96,768]{2,1,0:T(8,128)} %collective-permute-done.6.r_6_.r_12_.r_8_), channel_id=1, source_target_pairs={{0,4},{4,0},{8,12},{12,8},{16,20},{20,16},{24,28},{28,24},{1,5},{5... | collective-permute-start | bytes 2654216 | tf_op jit(solution)/shard_map/ppermute | solution.py:646
  61.1 17.8 %collective-permute-start.11 = (f32[3,96,768]{2,1,0:T(8,128)}, f32[3,96,768]{2,1,0:T(8,128)}, u32[]{:S(2)}, u32[]{:S(2)}) collective-permute-start(f32[3,96,768]{2,1,0:T(8,128)} %collective-permute-done.7.r_7_.r_13_.r_9_), channel_id=1, source_target_pairs={{0,4},{4,0},{8,12},{12,8},{16,20},{20,16},{24,28},{28,24},{1,5},{5... | collective-permute-start | bytes 2654216 | tf_op jit(solution)/shard_map/ppermute | solution.py:646
  70.3 25.2 %copy-start.5 = (f32[2,96,768]{2,1,0:T(8,128)}, f32[2,96,768]{2,1,0:T(8,128)S(1)}, u32[]{:S(2)}) copy-start(f32[2,96,768]{2,1,0:T(8,128)S(1)} %collective-permute-done.2) | copy-start | bytes 1769476
  71.3 7.5 %collective-permute-start.12 = (f32[3,96,768]{2,1,0:T(8,128)}, f32[3,96,768]{2,1,0:T(8,128)}, u32[]{:S(2)}, u32[]{:S(2)}) collective-permute-start(f32[3,96,768]{2,1,0:T(8,128)} %collective-permute-done.8.r_8_.r_14_.r_10_), channel_id=1, source_target_pairs={{0,4},{4,0},{8,12},{12,8},{16,20},{20,16},{24,28},{28,24},{1,5},{5... | collective-permute-start | bytes 2654216 | tf_op jit(solution)/shard_map/ppermute | solution.py:646
  71.3 29.6 %collective-permute-start.1 = (f32[2,96,768]{2,1,0:T(8,128)S(1)}, f32[2,96,768]{2,1,0:T(8,128)S(1)}, u32[]{:S(2)}, u32[]{:S(2)}) collective-permute-start(f32[2,96,768]{2,1,0:T(8,128)S(1)} %maximum_convert_fusion), channel_id=1, source_target_pairs={{0,2},{1,3},{2,0},{3,1},{4,6},{5,7},{6,4},{7,5},{8,10},{9,11},{10,... | collective-permute-start | bytes 1769480 | tf_op jit(solution)/shard_map/ppermute | solution.py:630
  100.9 0.8 copy-start.6
  103.1 42.4 %copy-start.2 = (f32[3,192,768]{2,1,0:T(8,128)}, f32[3,192,768]{2,1,0:T(8,128)S(1)}, u32[]{:S(2)}) copy-start(f32[3,192,768]{2,1,0:T(8,128)S(1)} %pad_maximum_fusion.r_19_) | copy-start | bytes 5308420
  103.1 41.6 %collective-permute-start.14 = (f32[3,192,768]{2,1,0:T(8,128)S(1)}, f32[3,192,768]{2,1,0:T(8,128)}, u32[]{:S(2)}, u32[]{:S(2)}) collective-permute-start(f32[3,192,768]{2,1,0:T(8,128)S(1)} %pad_maximum_fusion.r_19_), channel_id=1, source_target_pairs={{0,16},{4,12},{8,24},{12,4},{16,0},{20,28},{24,8},{28,20},{1,17},{... | collective-permute-start | bytes 5308424 | tf_op jit(solution)/shard_map/ppermute | solution.py:640
  104.7 40.0 %collective-permute-start.13 = (f32[3,192,768]{2,1,0:T(8,128)S(1)}, f32[3,192,768]{2,1,0:T(8,128)}, u32[]{:S(2)}, u32[]{:S(2)}) collective-permute-start(f32[3,192,768]{2,1,0:T(8,128)S(1)} %pad_maximum_fusion.r_19_), channel_id=1, source_target_pairs={{0,8},{4,20},{8,0},{12,28},{16,24},{20,4},{24,16},{28,12},{1,9},{5... | collective-permute-start | bytes 5308424 | tf_op jit(solution)/shard_map/ppermute | solution.py:640
  121.7 46.0 %copy-start.11 = (bf16[2,768]{1,0:T(2,128)(2,1)S(1)}, bf16[2,768]{1,0:T(2,128)(2,1)}, u32[]{:S(2)}) copy-start(bf16[2,768]{1,0:T(2,128)(2,1)} %param.25) | copy-start | bytes 9220
  121.7 46.0 %copy-start.12 = (bf16[2,768]{1,0:T(2,128)(2,1)S(1)}, bf16[2,768]{1,0:T(2,128)(2,1)}, u32[]{:S(2)}) copy-start(bf16[2,768]{1,0:T(2,128)(2,1)} %param.24) | copy-start | bytes 9220
  121.7 46.0 %copy-start.13 = (bf16[2,768]{1,0:T(2,128)(2,1)S(1)}, bf16[2,768]{1,0:T(2,128)(2,1)}, u32[]{:S(2)}) copy-start(bf16[2,768]{1,0:T(2,128)(2,1)} %param.23) | copy-start | bytes 9220
  121.7 46.6 %slice-start = ((f32[104,768]{1,0:T(8,128)}), f32[1,768]{1,0:T(1,128)S(1)}, s32[]{:S(2)}) async-start(f32[104,768]{1,0:T(8,128)} %copy-done.7), calls=%async_computation | async-start | bytes 6144 | tf_op jit(solution)/shard_map/slice | solution.py:761
  121.7 46.6 %slice-start.1 = ((f32[104,768]{1,0:T(8,128)}), f32[1,768]{1,0:T(1,128)S(1)}, s32[]{:S(2)}) async-start(f32[104,768]{1,0:T(8,128)} %copy-done.8), calls=%async_computation.1 | async-start | bytes 6144 | tf_op jit(solution)/shard_map/slice | solution.py:761
  121.8 46.6 %slice-start.2 = ((f32[104,768]{1,0:T(8,128)}), f32[1,768]{1,0:T(1,128)S(1)}, s32[]{:S(2)}) async-start(f32[104,768]{1,0:T(8,128)} %copy-done.9), calls=%async_computation.2 | async-start | bytes 6144 | tf_op jit(solution)/shard_map/slice | solution.py:761
  144.8 22.8 %collective-permute-start.15 = (f32[3,192,768]{2,1,0:T(8,128)}, f32[3,192,768]{2,1,0:T(8,128)}, u32[]{:S(2)}, u32[]{:S(2)}) collective-permute-start(f32[3,192,768]{2,1,0:T(8,128)} %collective-permute-done.13.r_20_), channel_id=1, source_target_pairs={{0,16},{4,12},{8,24},{12,4},{16,0},{20,28},{24,8},{28,20},{1,17},{... | collective-permute-start | bytes 5308424 | tf_op jit(solution)/shard_map/ppermute | solution.py:643
  145.5 23.5 %collective-permute-start.17 = (f32[3,192,768]{2,1,0:T(8,128)}, f32[3,192,768]{2,1,0:T(8,128)}, u32[]{:S(2)}, u32[]{:S(2)}) collective-permute-start(f32[3,192,768]{2,1,0:T(8,128)} %collective-permute-done.13.r_20_), channel_id=1, source_target_pairs={{0,4},{4,0},{8,12},{12,8},{16,20},{20,16},{24,28},{28,24},{1,5},{5... | collective-permute-start | bytes 5308424 | tf_op jit(solution)/shard_map/ppermute | solution.py:646
  145.5 23.5 %collective-permute-start.16 = (f32[3,192,768]{2,1,0:T(8,128)S(1)}, f32[3,192,768]{2,1,0:T(8,128)}, u32[]{:S(2)}, u32[]{:S(2)}) collective-permute-start(f32[3,192,768]{2,1,0:T(8,128)S(1)} %pad_maximum_fusion.r_19_), channel_id=1, source_target_pairs={{0,4},{4,0},{8,12},{12,8},{16,20},{20,16},{24,28},{28,24},{1,5},{5... | collective-permute-start | bytes 5308424 | tf_op jit(solution)/shard_map/ppermute | solution.py:646
  146.0 23.0 %collective-permute-start.18 = (f32[3,192,768]{2,1,0:T(8,128)}, f32[3,192,768]{2,1,0:T(8,128)}, u32[]{:S(2)}, u32[]{:S(2)}) collective-permute-start(f32[3,192,768]{2,1,0:T(8,128)} %collective-permute-done.14.r_21_), channel_id=1, source_target_pairs={{0,4},{4,0},{8,12},{12,8},{16,20},{20,16},{24,28},{28,24},{1,5},{5... | collective-permute-start | bytes 5308424 | tf_op jit(solution)/shard_map/ppermute | solution.py:646
  167.6 4.0 %collective-permute-start.19 = (f32[3,192,768]{2,1,0:T(8,128)}, f32[3,192,768]{2,1,0:T(8,128)}, u32[]{:S(2)}, u32[]{:S(2)}) collective-permute-start(f32[3,192,768]{2,1,0:T(8,128)} %collective-permute-done.15.r_22_), channel_id=1, source_target_pairs={{0,4},{4,0},{8,12},{12,8},{16,20},{20,16},{24,28},{28,24},{1,5},{5... | collective-permute-start | bytes 5308424 | tf_op jit(solution)/shard_map/ppermute | solution.py:646
  260.6 24.9 %collective-permute-start.20 = (f32[1,4,96,1920]{3,2,1,0:T(8,128)}, f32[1,4,96,1920]{3,2,1,0:T(8,128)S(1)}, u32[]{:S(2)}, u32[]{:S(2)}) collective-permute-start(f32[1,4,96,1920]{3,2,1,0:T(8,128)} %dynamic-slice_bitcast_fusion), channel_id=1, source_target_pairs={{0,4},{4,0},{8,12},{12,8},{16,20},{20,16},{24,28},{28,24},{1,5},{5... | collective-permute-start | bytes 8847368 | tf_op jit(solution)/shard_map/ppermute | solution.py:646
  285.1 35.2 %collective-permute-start.22 = (f32[1,4,96,768]{3,2,1,0:T(8,128)}, f32[1,4,96,768]{3,2,1,0:T(8,128)}, u32[]{:S(2)}, u32[]{:S(2)}) collective-permute-start(f32[1,4,96,768]{3,2,1,0:T(8,128)} %dynamic-slice_bitcast_fusion.1), channel_id=1, source_target_pairs={{0,4},{4,0},{8,12},{12,8},{16,20},{20,16},{24,28},{28,24},{1,5},{5... | collective-permute-start | bytes 3538952 | tf_op jit(solution)/shard_map/ppermute | solution.py:646
  289.1 31.3 %collective-permute-start.21 = (f32[1,2,96,1920]{3,2,1,0:T(8,128)}, f32[1,2,96,1920]{3,2,1,0:T(8,128)}, u32[]{:S(2)}, u32[]{:S(2)}) collective-permute-start(f32[1,2,96,1920]{3,2,1,0:T(8,128)} %pad_maximum_fusion.2), channel_id=1, source_target_pairs={{0,8},{4,20},{8,0},{12,28},{16,24},{20,4},{24,16},{28,12},{1,9},{5... | collective-permute-start | bytes 4423688 | tf_op jit(solution)/shard_map/ppermute | solution.py:665
  289.9 30.5 %copy-start.1 = (f32[8,96,768]{2,1,0:T(8,128)S(1)}, f32[8,96,768]{2,1,0:T(8,128)}, u32[]{:S(2)}) copy-start(f32[8,96,768]{2,1,0:T(8,128)} %dynamic_update_slice.3) | copy-start | bytes 7077892
  322.8 35.0 %collective-permute-start.24 = (f32[1,2,96,768]{3,2,1,0:T(8,128)}, f32[1,2,96,768]{3,2,1,0:T(8,128)S(1)}, u32[]{:S(2)}, u32[]{:S(2)}) collective-permute-start(f32[1,2,96,768]{3,2,1,0:T(8,128)} %pad_maximum_fusion.4), channel_id=1, source_target_pairs={{0,8},{4,20},{8,0},{12,28},{16,24},{20,4},{24,16},{28,12},{1,9},{5... | collective-permute-start | bytes 1769480 | tf_op jit(solution)/shard_map/ppermute | solution.py:665
  325.7 32.1 %collective-permute-start.23 = (f32[1,96,1920]{2,1,0:T(8,128)S(1)}, f32[1,96,1920]{2,1,0:T(8,128)}, u32[]{:S(2)}, u32[]{:S(2)}) collective-permute-start(f32[1,96,1920]{2,1,0:T(8,128)S(1)} %dynamic-slice_bitcast_fusion.2), channel_id=1, source_target_pairs={{0,16},{4,12},{8,24},{12,4},{16,0},{20,28},{24,8},{28,20},{1,17},{... | collective-permute-start | bytes 2211848 | tf_op jit(solution)/shard_map/ppermute | solution.py:672
  359.1 6.8 %collective-permute-start.25 = (f32[1,96,768]{2,1,0:T(8,128)S(1)}, f32[1,96,768]{2,1,0:T(8,128)S(1)}, u32[]{:S(2)}, u32[]{:S(2)}) collective-permute-start(f32[1,96,768]{2,1,0:T(8,128)S(1)} %dynamic-slice_bitcast_fusion.3), channel_id=1, source_target_pairs={{0,16},{4,12},{8,24},{12,4},{16,0},{20,28},{24,8},{28,20},{1,17},{... | collective-permute-start | bytes 884744 | tf_op jit(solution)/shard_map/ppermute | solution.py:672
where the time goes:
time: 374 us; the launch traced here: 368 us
  Pallas kernels  231 us (62%)
  waiting for transfers between devices  70.8 us (19%)
  starting transfers between devices  24.8 us (7%)
  local copies, waits for them, and re-layouts  23.5 us (6%)
  other arithmetic  16.1 us (4%)
    pallas_call x1, Pallas kernels, ffn_block(): pl.pallas_call(lambda *r: ffn_kernel(*r, long0=long0, hw=hw), grid_spec=p...  85.3 us
    pallas_call x4, Pallas kernels, attn_fwd(): pl.pallas_call(lambda *r: attn_fwd_kernel(*r, slot=slot, nshort=nshort, s...  65.8 us
    pallas_call x2, Pallas kernels, bwd_rest(): pl.pallas_call(lambda *r: bwd_rest_kernel(*r, lo=lo, blk=blk, **kw), grid...  61.7 us
    ppermute x6, waiting for transfers between devices, along_tensor(): lax.ppermute(piece, 'tensor', [(i, (i + s) % n) for i in range(n)])  35.4 us
    ppermute x2, waiting for transfers between devices, second_hop(): return lax.ppermute(a, 'dp', self.second)  22.5 us
    pallas_call x1, Pallas kernels, bwd_own(): pl.pallas_call(lambda *r: bwd_own_kernel(*r, blk=blk, **kw), grid=(rows /...  18.4 us
    ppermute x6, starting transfers between devices, along_tensor(): lax.ppermute(piece, 'tensor', [(i, (i + s) % n) for i in range(n)])  10.5 us
  transfers between devices with their start and end apart: 26, of which 10 were waited for; matrix products, arithmetic and copies ran while one was open for 7% of the time, Pallas kernels for 40%

commit v1 on v0

--- a/solution.py
+++ b/solution.py
@@ -65,9 +65,9 @@
 
 
 def attn_fwd_kernel(
-    len_ref, place_ref, xs_ref, xl_ref, b_ref, *refs, slot, nshort, short_slot, heads, blk
+    len_ref, place_ref, slot_ref, xs_ref, xl_ref, b_ref, *refs, own, nshort, short_slot, heads, blk
 ):
-    if slot:
+    if not own:
         pieces, (p_ref, o_ref, w_s, x_s, stage, sems) = refs[:8], refs[-6:]
     else:
         w_ref, p_ref, o_ref, w_s, x_s = refs
@@ -78,9 +78,10 @@
 
     @pl.when(b == 0)
     def _():
-        if slot:
+        if not own:
+            at = slot_ref[0] - 1
             copies = [
-                pltpu.make_async_copy(pieces[n].at[slot - 1], stage.at[n], sems.at[n])
+                pltpu.make_async_copy(pieces[n].at[at], stage.at[n], sems.at[n])
                 for n in range(8)
             ]
             for c in copies:
@@ -136,8 +137,9 @@
 
     @pl.when(b < long0)
     def _():
-        for i in range(sub):
-            pair(i * short_slot, short_slot, len_ref[b * sub + i])
+        @pl.loop(0, sub)
+        def _(i):
+            pair(pl.multiple_of(i * short_slot, short_slot), short_slot, len_ref[b * sub + i])
 
     @pl.when(b >= long0)
     def _():
@@ -153,7 +155,7 @@
     if slot:
         in_specs += [pl.BlockSpec(memory_space=pl.ANY)] * 10
         args += list(w) + list(prev)
-        aliases = {13: 0, 14: 1}
+        aliases = {14: 0, 15: 1}
         r = w[0].shape[1]
         scratch += [pltpu.VMEM((8, r, d), F32), pltpu.SemaphoreType.DMA((8,))]
     else:
@@ -161,15 +163,15 @@
         args.append(w)
     return pl.pallas_call(
         lambda *r: attn_fwd_kernel(
-            *r, slot=slot, nshort=nshort, short_slot=short_slot, heads=heads, blk=blk
+            *r, own=slot == 0, nshort=nshort, short_slot=short_slot, heads=heads, blk=blk
         ),
         grid_spec=pltpu.PrefetchScalarGridSpec(
-            num_scalar_prefetch=2,
+            num_scalar_prefetch=3,
             grid=(rows // blk,),
             in_specs=in_specs,
             out_specs=[
-                pl.BlockSpec((1, blk, 768), lambda b, *_: (slot, b, 0)),
-                pl.BlockSpec((1, blk, 256), lambda b, *_: (slot, b, 0)),
+                pl.BlockSpec((1, blk, 768), lambda b, ln, at, sl: (sl[0], b, 0)),
+                pl.BlockSpec((1, blk, 256), lambda b, ln, at, sl: (sl[0], b, 0)),
             ],
             scratch_shapes=scratch,
         ),
@@ -181,7 +183,7 @@
         compiler_params=pltpu.CompilerParams(vmem_limit_bytes=60 * 2**20),
         cost_estimate=pl.CostEstimate(flops=14 * 10**9, bytes_accessed=2**23, transcendentals=0),
         name="attn_fwd",
-    )(lens, place, *args)
+    )(lens, place, jnp.full((1,), slot, jnp.int32), *args)
 
 
 def attn_bwd_pair(refs, sl, rows, heads):
@@ -229,8 +231,9 @@
 
     @pl.when(b < long0)
     def _():
-        for i in range(sub):
-            one(i * short_slot, short_slot)
+        @pl.loop(0, sub)
+        def _(i):
+            one(pl.multiple_of(i * short_slot, short_slot), short_slot)
 
     @pl.when(b >= long0)
     def _():
@@ -746,16 +749,26 @@
         c1 = wires.second_hop(after(a1, z2[0]))
         w1 = [t1, a1, b1, c1]
         w1 += [wires.to_pair(x) for x in w1[:3]] + [wires.to_pair(after(c1, z2[2]))]
+        def eighths(*x):
+            return wires.whole_eighth(jnp.stack(x)).reshape(len(x), -1, d)
+
+        t2 = eighths(z2[0], z2[2])
+        a2, b2 = wires.first_hop(t2)
         for s in range(1, n_tensor):
             po = attn_fwd(s, lens, place, xs, xl, w1, bias_of(z[s - 1]), po, slots=n_tensor, **kw)
             if s == 1:
-                *z2, p, o = lax.optimization_barrier((*z2, *po))
-                po = p, o
-                t2 = wires.whole_eighth(jnp.stack(z2))
-                t2 = t2.reshape(n_tensor - 1, -1, d)
-                a2, b2 = wires.first_hop(t2)
-        t2, a2, b2, *po = lax.optimization_barrier((t2, a2, b2, *po))
-        w2 = [t2, a2, b2, wires.second_hop(a2)]
+                a2, b2, mid, *po = lax.optimization_barrier((a2, b2, z2[1], *po))
+                t2b = eighths(mid)
+                a2b, b2b = wires.first_hop(t2b)
+            if s == 2:
+                a2b, b2b, *po = lax.optimization_barrier((a2b, b2b, *po))
+                t2, a2, b2 = [
+                    jnp.concatenate([u[:1], v, u[1:]], 0)
+                    for u, v in ((t2, t2b), (a2, a2b), (b2, b2b))
+                ]
+                c2 = wires.second_hop(a2)
+        c2, *po = lax.optimization_barrier((c2, *po))
+        w2 = [t2, a2, b2, c2]
         w2 += [wires.to_pair(x) for x in w2]
         p, o = po
         bup = jnp.stack([x[0] for x in [small] + z])

time: 374 us -> 360 us (0.963)
  waiting for transfers between devices: 70.8 us -> 44.2 us
  other arithmetic: 16.1 us -> 23.2 us
  starting transfers between devices: 24.8 us -> 30.1 us
  Pallas kernels: 231 us -> 235 us
    ppermute x2, waiting for transfers between devices: 22.5 us -> 0.01 us  [second_hop(): return lax.ppermute(a, 'dp', self.second)]
    concatenate x0 -> x3, other arithmetic: none -> 6.55 us  [on_device(): jnp.concatenate([u[:1], v, u[1:]], 0)]
  transfers between devices with their start and end apart: 26 -> 28, of which waited for: 10 -> 8; matrix products, arithmetic and copies ran while one was open for 7% -> 9% of each run, Pallas kernels for 40% -> 42%
where the time goes in v1:
time: 360 us; the launch traced here: 355 us
  Pallas kernels  235 us (65%)
  waiting for transfers between devices  44.2 us (12%)
  starting transfers between devices  30.1 us (8%)
  other arithmetic  23.2 us (6%)
  local copies, waits for them, and re-layouts  20.6 us (6%)
    pallas_call x1, Pallas kernels, ffn_block(): pl.pallas_call(lambda *r: ffn_kernel(*r, long0=long0, hw=hw), grid_spec=p...  85.4 us
    pallas_call x4, Pallas kernels, attn_fwd(): pl.pallas_call(lambda *r: attn_fwd_kernel(*r, own=slot == 0, nshort=nshor...  67.7 us
    pallas_call x2, Pallas kernels, bwd_rest(): pl.pallas_call(lambda *r: bwd_rest_kernel(*r, lo=lo, blk=blk, **kw), grid...  63 us
    ppermute x6, waiting for transfers between devices, along_tensor(): lax.ppermute(piece, 'tensor', [(i, (i + s) % n) for i in range(n)])  34.4 us
    pallas_call x1, Pallas kernels, bwd_own(): pl.pallas_call(lambda *r: bwd_own_kernel(*r, blk=blk, **kw), grid=(rows /...  19.2 us
    ppermute x6, starting transfers between devices, along_tensor(): lax.ppermute(piece, 'tensor', [(i, (i + s) % n) for i in range(n)])  9.99 us
  transfers between devices with their start and end apart: 28, of which 8 were waited for; matrix products, arithmetic and copies ran while one was open for 9% of the time, Pallas kernels for 42%

profile of v1, /device:TPU:0, one launch (start us, length us, event | category | flops | bytes accessed | tf_op | source)
XLA Modules:
  0.0 354.7 jit_solution(5694337831021006869)
XLA Ops:
  2.3 1.0 fusion.2
  3.4 5.1 %collective-permute-start.7 = (f32[104,768]{1,0:T(8,128)S(1)}, f32[104,768]{1,0:T(8,128)S(1)}, u32[]{:S(2)}, u32[]{:S(2)}) collective-permute-start(f32[104,768]{1,0:T(8,128)S(1)} %pad_maximum_fusion.8), channel_id=1, source_target_pairs={{0,3},{1,0},{2,1},{3,2},{4,7},{5,4},{6,5},{7,6},{8,11},{9,8},{10,9... | collective-permute-start | bytes 958472 | tf_op jit(solution)/shard_map/ppermute | solution.py:633
  8.6 1.0 collective-permute-start.5
  9.7 1.1 pad_maximum_fusion.3.r_6_.r_8_
  12.8 16.0 %attn_fwd.4 = (bf16[4,2048,768]{2,1,0:T(8,128)(2,1)}, bf16[4,2048,256]{2,1,0:T(8,128)(2,1)}) custom-call(s32[5]{0:T(128)} %pad_add_fusion.1.r_0_, s32[3,8]{1,0:T(4,128)} %pad_add_fusion.r_1_.r_0_, s32[1]{0:T(128)} %constant.96.clone.1.r_2_, bf16[512,768]{1,0:T(8,128)(2,1)} %bitcast.104, bf16[1536,768]{1,0:T(8,128)(2,1)} %bitcast.97, ...), custom_call_target="tpu_custom_call" | custom-call | flops 14000000000 | bytes 8388608 | tf_op jit(solution)/shard_map/attn_fwd/pallas_call | solution.py:164
  28.9 7.0 %collective-permute-done.6 = f32[104,768]{1,0:T(8,128)S(1)} collective-permute-done((f32[104,768]{1,0:T(8,128)S(1)}, f32[104,768]{1,0:T(8,128)S(1)}, u32[]{:S(2)}, u32[]{:S(2)}) %collective-permute-start.6) | collective-permute-done | bytes 319520 | tf_op jit(solution)/shard_map/ppermute | solution.py:633
  36.0 1.6 collective-permute-start.8
  37.5 1.0 dynamic-slice_bitcast_fusion.4
  38.5 0.9 maximum_convert_fusion
  39.4 0.8 collective-permute-start
  40.2 1.5 collective-permute-start.9
  41.7 13.6 %collective-permute-done = f32[2,96,768]{2,1,0:T(8,128)S(1)} collective-permute-done((f32[2,96,768]{2,1,0:T(8,128)}, f32[2,96,768]{2,1,0:T(8,128)S(1)}, u32[]{:S(2)}, u32[]{:S(2)}) %collective-permute-start) | collective-permute-done | bytes 589856 | tf_op jit(solution)/shard_map/ppermute | solution.py:633
  55.4 1.3 collective-permute-done.8.r_7_.r_12_.r_8_
  56.7 2.5 collective-permute-start.10
  60.1 11.0 %collective-permute-done.1 = f32[2,96,768]{2,1,0:T(8,128)S(1)} collective-permute-done((f32[2,96,768]{2,1,0:T(8,128)}, f32[2,96,768]{2,1,0:T(8,128)S(1)}, u32[]{:S(2)}, u32[]{:S(2)}) %collective-permute-start.1) | collective-permute-done | bytes 589856 | tf_op jit(solution)/shard_map/ppermute | solution.py:633
  71.0 2.8 collective-permute-start.4
  76.1 1.1 pad_maximum_fusion.5
  77.2 2.1 collective-permute-start.3
  79.3 1.5 collective-permute-start.2
  80.8 17.1 %attn_fwd.5 = (bf16[4,2048,768]{2,1,0:T(8,128)(2,1)}, bf16[4,2048,256]{2,1,0:T(8,128)(2,1)}) custom-call(s32[5]{0:T(128)} %pad_add_fusion.1.r_0_, s32[3,8]{1,0:T(4,128)} %pad_add_fusion.r_1_.r_0_, s32[1]{0:T(128)} %constant.99.clone.1.r_2_, bf16[512,768]{1,0:T(8,128)(2,1)} %bitcast.105, ...), custom_call_target="tpu_custom_call", output_to_operand_aliasing={{0}: (14, {}), {1}: (15, {})} | custom-call | flops 14000000000 | bytes 8388608 | tf_op jit(solution)/shard_map/attn_fwd/pallas_call | solution.py:164
  97.9 2.9 collective-permute-done.4
  100.8 4.7 %collective-permute-done.3 = f32[2,192,768]{2,1,0:T(8,128)S(1)} collective-permute-done((f32[2,192,768]{2,1,0:T(8,128)}, f32[2,192,768]{2,1,0:T(8,128)S(1)}, u32[]{:S(2)}, u32[]{:S(2)}) %collective-permute-start.3) | collective-permute-done | bytes 1179680 | tf_op jit(solution)/shard_map/ppermute | solution.py:643
  105.6 2.3 collective-permute-start.16
  107.8 1.5 collective-permute-start.15
  109.3 17.1 %attn_fwd.6 = (bf16[4,2048,768]{2,1,0:T(8,128)(2,1)}, bf16[4,2048,256]{2,1,0:T(8,128)(2,1)}) custom-call(s32[5]{0:T(128)} %pad_add_fusion.1.r_0_, s32[3,8]{1,0:T(4,128)} %pad_add_fusion.r_1_.r_0_, s32[1]{0:T(128)} %constant.100.clone.1.r_2_, bf16[512,768]{1,0:T(8,128)(2,1)} %bitcast.106, ...), custom_call_target="tpu_custom_call", output_to_operand_aliasing={{0}: (14, {}), {1}: (15, {})} | custom-call | flops 14000000000 | bytes 8388608 | tf_op jit(solution)/shard_map/attn_fwd/pallas_call | solution.py:164
  126.6 1.2 pad_maximum_fusion.r_20_
  128.2 3.0 pad_maximum_fusion.1.r_19_
  131.9 2.4 pad_maximum_fusion.2.r_21_
  134.4 17.4 %attn_fwd.7 = (bf16[4,2048,768]{2,1,0:T(8,128)(2,1)}, bf16[4,2048,256]{2,1,0:T(8,128)(2,1)}) custom-call(s32[5]{0:T(128)} %pad_add_fusion.1.r_0_, s32[3,8]{1,0:T(4,128)} %pad_add_fusion.r_1_.r_0_, s32[1]{0:T(128)} %constant.101.clone.1.r_2_, bf16[512,768]{1,0:T(8,128)(2,1)} %bitcast.107, ...), custom_call_target="tpu_custom_call", output_to_operand_aliasing={{0}: (14, {}), {1}: (15, {})} | custom-call | flops 14000000000 | bytes 8388608 | tf_op jit(solution)/shard_map/attn_fwd/pallas_call | solution.py:164
  153.8 2.3 collective-permute-done.21.r_26_
  156.0 85.4 %ffn_block.1 = (bf16[512,768]{1,0:T(8,128)(2,1)}, bf16[1536,768]{1,0:T(8,128)(2,1)}, f32[2048,768]{1,0:T(8,128)}, bf16[4,2048,256]{2,1,0:T(8,128)(2,1)}, f32[768,1920]{1,0:T(8,128)}) custom-call(s32[3,8]{1,0:T(4,128)} %pad_add_fusion.r_1_.r_0_, bf16[512,768]{1,0:T(8,128)(2,1)} %bitcast.108, bf16[1536,768]{1,0:T(8,128)(2,1)} %bitcast.101, ...), custom_call_target="tpu_custom_call" | custom-call | flops 80000000000 | bytes 33554432 | tf_op jit(solution)/shard_map/ffn_block/pallas_call | solution.py:563
  241.4 3.6 %dynamic-slice_bitcast_fusion = f32[1,4,96,1920]{3,2,1,0:T(8,128)} fusion(f32[1,4,2,96,1920]{4,3,2,1,0:T(8,128)} %bitcast.74, s32[]{:T(128)S(6)} %select_n.114), kind=kLoop, calls=%fused_computation.1 | loop fusion | bytes 5898244 | tf_op jit(solution)/shard_map/jit(dynamic_index_in_dim)/squeeze | solution.py:657
  245.4 19.2 %attn_bwd_own.1 = (bf16[2048,768]{1,0:T(8,128)(2,1)}, f32[768,768]{1,0:T(8,128)}, f32[8,768]{1,0:T(8,128)}) custom-call(bf16[512,768]{1,0:T(8,128)(2,1)} %bitcast.109, bf16[1536,768]{1,0:T(8,128)(2,1)} %bitcast.102, bf16[4,2048,768]{2,1,0:T(8,128)(2,1)} %get-tuple-element.79.r_2_.r_1_, bf16[4,2048,256]{2,1,0:T(8,128)(2,1)} %get-tuple-element.73.r_5_.r_3_.r_2_, ...), custom_call_target="tpu_custom_call" | custom-call | flops 17999998976 | bytes 8388608 | tf_op jit(solution)/shard_map/attn_bwd_own/pallas_call | solution.py:270
  265.5 2.6 dynamic_update_slice.3
  268.1 2.4 dynamic-slice_bitcast_fusion.1
  270.6 2.1 bitcast_add_fusion
  273.0 1.3 pad_maximum_fusion.4
  274.7 31.7 %attn_bwd_rest.2 = (f32[512,768]{1,0:T(8,128)}, f32[1536,768]{1,0:T(8,128)}) custom-call(s32[3,8]{1,0:T(4,128)} %pad_add_fusion.r_1_.r_0_, bf16[4,2048,768]{2,1,0:T(8,128)(2,1)} %get-tuple-element.79.r_2_.r_1_, bf16[4,2048,256]{2,1,0:T(8,128)(2,1)} %get-tuple-element.73.r_5_.r_3_.r_2_, bf16[4,2048,256]{2,1,0:T(8,128)(2,1)} %get-tuple-element.80.r_4_.r_3_, ...), custom_call_target="tpu_custom_call" | custom-call | flops 24999999488 | bytes 8388608 | tf_op jit(solution)/shard_map/attn_bwd_rest/pallas_call | solution.py:372
  306.4 1.4 bitcast_add_fusion.1
  307.9 0.9 pad_maximum_fusion.7
  308.8 1.7 collective-permute-start.26
  310.4 1.5 maximum_add_fusion
  312.0 1.2 collective-permute-start.25
  313.2 31.3 %attn_bwd_rest.3 = f32[1536,768]{1,0:T(8,128)} custom-call(s32[3,8]{1,0:T(4,128)} %pad_add_fusion.r_1_.r_0_, bf16[4,2048,768]{2,1,0:T(8,128)(2,1)} %get-tuple-element.79.r_2_.r_1_, bf16[4,2048,256]{2,1,0:T(8,128)(2,1)} %get-tuple-element.73.r_5_.r_3_.r_2_, bf16[4,2048,256]{2,1,0:T(8,128)(2,1)} %get-tuple-element.80.r_4_.r_3_, ...), custom_call_target="tpu_custom_call", output_to_operand_aliasing={{}: (15, {})} | custom-call | flops 24999999488 | bytes 8388608 | tf_op jit(solution)/shard_map/attn_bwd_rest/pallas_call | solution.py:372
  344.6 1.2 fusion
  345.9 1.1 collective-permute-start.27
  350.4 0.8 slice_bitcast_fusion.1
  351.3 1.4 collective-permute-done.27
  (137 shorter events, 17.8 us)
Async XLA Ops:
  0.6 9.0 %copy-start.3 = (bf16[192,768]{1,0:T(8,128)(2,1)S(1)}, bf16[192,768]{1,0:T(8,128)(2,1)}, u32[]{:S(2)}) copy-start(bf16[192,768]{1,0:T(8,128)(2,1)} %param.22) | copy-start | bytes 884740
  0.7 9.0 %copy-start = (bf16[3,768,192]{1,2,0:T(8,128)(2,1)S(1)}, bf16[3,768,192]{1,2,0:T(8,128)(2,1)}, u32[]{:S(2)}) copy-start(bf16[3,768,192]{1,2,0:T(8,128)(2,1)} %param.20) | copy-start | bytes 2654212
  3.3 7.6 %copy-start.10 = (f32[64]{0:T(128)S(1)}, f32[64]{0:T(128)}, u32[]{:S(2)}) copy-start(f32[64]{0:T(128)} %constant.102.clone) | copy-start | bytes 772
  3.3 8.3 %copy-start.14 = (s32[3]{0:T(128)S(1)}, s32[3]{0:T(128)}, u32[]{:S(2)}) copy-start(s32[3]{0:T(128)} %param.19) | copy-start | bytes 40
  3.3 8.3 %copy-start.15 = (s32[2]{0:T(128)S(1)}, s32[2]{0:T(128)}, u32[]{:S(2)}) copy-start(s32[2]{0:T(128)} %param.17) | copy-start | bytes 28
  3.4 25.4 %collective-permute-start.7 = (f32[104,768]{1,0:T(8,128)S(1)}, f32[104,768]{1,0:T(8,128)S(1)}, u32[]{:S(2)}, u32[]{:S(2)}) collective-permute-start(f32[104,768]{1,0:T(8,128)S(1)} %pad_maximum_fusion.8), channel_id=1, source_target_pairs={{0,3},{1,0},{2,1},{3,2},{4,7},{5,4},{6,5},{7,6},{8,11},{9,8},{10,9... | collective-permute-start | bytes 958472 | tf_op jit(solution)/shard_map/ppermute | solution.py:633
  8.6 27.2 %collective-permute-start.6 = (f32[104,768]{1,0:T(8,128)S(1)}, f32[104,768]{1,0:T(8,128)S(1)}, u32[]{:S(2)}, u32[]{:S(2)}) collective-permute-start(f32[104,768]{1,0:T(8,128)S(1)} %pad_maximum_fusion.8), channel_id=1, source_target_pairs={{0,2},{1,3},{2,0},{3,1},{4,6},{5,7},{6,4},{7,5},{8,10},{9,11},{10,... | collective-permute-start | bytes 958472 | tf_op jit(solution)/shard_map/ppermute | solution.py:633
  8.6 27.3 %collective-permute-start.5 = (f32[104,768]{1,0:T(8,128)S(1)}, f32[104,768]{1,0:T(8,128)S(1)}, u32[]{:S(2)}, u32[]{:S(2)}) collective-permute-start(f32[104,768]{1,0:T(8,128)S(1)} %pad_maximum_fusion.8), channel_id=1, source_target_pairs={{0,1},{1,2},{2,3},{3,0},{4,5},{5,6},{6,7},{7,4},{8,9},{9,10},{10,1... | collective-permute-start | bytes 958472 | tf_op jit(solution)/shard_map/ppermute | solution.py:633
  28.8 45.0 %copy-start.8 = (f32[104,768]{1,0:T(8,128)}, f32[104,768]{1,0:T(8,128)S(1)}, u32[]{:S(2)}) copy-start(f32[104,768]{1,0:T(8,128)S(1)} %collective-permute-done.7) | copy-start | bytes 958468
  35.8 38.8 %copy-start.9 = (f32[104,768]{1,0:T(8,128)}, f32[104,768]{1,0:T(8,128)S(1)}, u32[]{:S(2)}) copy-start(f32[104,768]{1,0:T(8,128)S(1)} %collective-permute-done.6) | copy-start | bytes 958468
  35.8 41.3 %copy-start.7 = (f32[104,768]{1,0:T(8,128)}, f32[104,768]{1,0:T(8,128)S(1)}, u32[]{:S(2)}) copy-start(f32[104,768]{1,0:T(8,128)S(1)} %collective-permute-done.5) | copy-start | bytes 958468
  36.0 41.2 %copy-start.6 = (f32[3,96,768]{2,1,0:T(8,128)}, f32[3,96,768]{2,1,0:T(8,128)S(1)}, u32[]{:S(2)}) copy-start(f32[3,96,768]{2,1,0:T(8,128)S(1)} %pad_maximum_fusion.6.r_6_.r_11_.r_7_) | copy-start | bytes 2654212
  36.0 20.7 %collective-permute-start.8 = (f32[3,96,768]{2,1,0:T(8,128)S(1)}, f32[3,96,768]{2,1,0:T(8,128)}, u32[]{:S(2)}, u32[]{:S(2)}) collective-permute-start(f32[3,96,768]{2,1,0:T(8,128)S(1)} %pad_maximum_fusion.6.r_6_.r_11_.r_7_), channel_id=1, source_target_pairs={{0,8},{4,20},{8,0},{12,28},{16,24},{20,4},{24,16},{28,12},{1,9},{5... | collective-permute-start | bytes 2654216 | tf_op jit(solution)/shard_map/ppermute | solution.py:643
  39.4 16.0 %collective-permute-start = (f32[2,96,768]{2,1,0:T(8,128)}, f32[2,96,768]{2,1,0:T(8,128)S(1)}, u32[]{:S(2)}, u32[]{:S(2)}) collective-permute-start(f32[2,96,768]{2,1,0:T(8,128)} %maximum_convert_fusion), channel_id=1, source_target_pairs={{0,1},{1,2},{2,3},{3,0},{4,5},{5,6},{6,7},{7,4},{8,9},{9,10},{10,1... | collective-permute-start | bytes 1769480 | tf_op jit(solution)/shard_map/ppermute | solution.py:633
  40.2 19.8 %collective-permute-start.9 = (f32[3,96,768]{2,1,0:T(8,128)S(1)}, f32[3,96,768]{2,1,0:T(8,128)}, u32[]{:S(2)}, u32[]{:S(2)}) collective-permute-start(f32[3,96,768]{2,1,0:T(8,128)S(1)} %pad_maximum_fusion.6.r_6_.r_11_.r_7_), channel_id=1, source_target_pairs={{0,16},{4,12},{8,24},{12,4},{16,0},{20,28},{24,8},{28,20},{1,17},{... | collective-permute-start | bytes 2654216 | tf_op jit(solution)/shard_map/ppermute | solution.py:643
  56.7 14.3 %collective-permute-start.10 = (f32[3,96,768]{2,1,0:T(8,128)}, f32[3,96,768]{2,1,0:T(8,128)}, u32[]{:S(2)}, u32[]{:S(2)}) collective-permute-start(f32[3,96,768]{2,1,0:T(8,128)} %collective-permute-done.8.r_7_.r_12_.r_8_), channel_id=1, source_target_pairs={{0,16},{4,12},{8,24},{12,4},{16,0},{20,28},{24,8},{28,20},{1,17},{... | collective-permute-start | bytes 2654216 | tf_op jit(solution)/shard_map/ppermute | solution.py:646
  59.2 11.8 %collective-permute-start.1 = (f32[2,96,768]{2,1,0:T(8,128)}, f32[2,96,768]{2,1,0:T(8,128)S(1)}, u32[]{:S(2)}, u32[]{:S(2)}) collective-permute-start(f32[2,96,768]{2,1,0:T(8,128)} %maximum_convert_fusion), channel_id=1, source_target_pairs={{0,3},{1,0},{2,1},{3,2},{4,7},{5,4},{6,5},{7,6},{8,11},{9,8},{10,9... | collective-permute-start | bytes 1769480 | tf_op jit(solution)/shard_map/ppermute | solution.py:633
  59.4 17.8 %collective-permute-start.11 = (f32[3,96,768]{2,1,0:T(8,128)S(1)}, f32[3,96,768]{2,1,0:T(8,128)}, u32[]{:S(2)}, u32[]{:S(2)}) collective-permute-start(f32[3,96,768]{2,1,0:T(8,128)S(1)} %pad_maximum_fusion.6.r_6_.r_11_.r_7_), channel_id=1, source_target_pairs={{0,4},{4,0},{8,12},{12,8},{16,20},{20,16},{24,28},{28,24},{1,5},{5... | collective-permute-start | bytes 2654216 | tf_op jit(solution)/shard_map/ppermute | solution.py:649
  59.5 21.3 %collective-permute-start.12 = (f32[3,96,768]{2,1,0:T(8,128)}, f32[3,96,768]{2,1,0:T(8,128)}, u32[]{:S(2)}, u32[]{:S(2)}) collective-permute-start(f32[3,96,768]{2,1,0:T(8,128)} %collective-permute-done.8.r_7_.r_12_.r_8_), channel_id=1, source_target_pairs={{0,4},{4,0},{8,12},{12,8},{16,20},{20,16},{24,28},{28,24},{1,5},{5... | collective-permute-start | bytes 2654216 | tf_op jit(solution)/shard_map/ppermute | solution.py:649
  60.0 19.3 %collective-permute-start.13 = (f32[3,96,768]{2,1,0:T(8,128)}, f32[3,96,768]{2,1,0:T(8,128)}, u32[]{:S(2)}, u32[]{:S(2)}) collective-permute-start(f32[3,96,768]{2,1,0:T(8,128)} %collective-permute-done.9.r_8_.r_13_.r_9_), channel_id=1, source_target_pairs={{0,4},{4,0},{8,12},{12,8},{16,20},{20,16},{24,28},{28,24},{1,5},{5... | collective-permute-start | bytes 2654216 | tf_op jit(solution)/shard_map/ppermute | solution.py:649
  71.0 9.7 %collective-permute-start.14 = (f32[3,96,768]{2,1,0:T(8,128)}, f32[3,96,768]{2,1,0:T(8,128)}, u32[]{:S(2)}, u32[]{:S(2)}) collective-permute-start(f32[3,96,768]{2,1,0:T(8,128)} %collective-permute-done.10.r_9_.r_14_.r_10_), channel_id=1, source_target_pairs={{0,4},{4,0},{8,12},{12,8},{16,20},{20,16},{24,28},{28,24},{1,5},{5... | collective-permute-start | bytes 2654216 | tf_op jit(solution)/shard_map/ppermute | solution.py:649
  71.0 29.8 %collective-permute-start.4 = (f32[2,96,768]{2,1,0:T(8,128)}, f32[2,96,768]{2,1,0:T(8,128)}, u32[]{:S(2)}, u32[]{:S(2)}) collective-permute-start(f32[2,96,768]{2,1,0:T(8,128)} %maximum_convert_fusion), channel_id=1, source_target_pairs={{0,2},{1,3},{2,0},{3,1},{4,6},{5,7},{6,4},{7,5},{8,10},{9,11},{10,... | collective-permute-start | bytes 1769480 | tf_op jit(solution)/shard_map/ppermute | solution.py:633
  77.2 28.3 %collective-permute-start.3 = (f32[2,192,768]{2,1,0:T(8,128)}, f32[2,192,768]{2,1,0:T(8,128)S(1)}, u32[]{:S(2)}, u32[]{:S(2)}) collective-permute-start(f32[2,192,768]{2,1,0:T(8,128)} %pad_maximum_fusion.5), channel_id=1, source_target_pairs={{0,16},{4,12},{8,24},{12,4},{16,0},{20,28},{24,8},{28,20},{1,17},{... | collective-permute-start | bytes 3538952 | tf_op jit(solution)/shard_map/ppermute | solution.py:643
  79.3 26.3 %collective-permute-start.2 = (f32[2,192,768]{2,1,0:T(8,128)}, f32[2,192,768]{2,1,0:T(8,128)S(1)}, u32[]{:S(2)}, u32[]{:S(2)}) collective-permute-start(f32[2,192,768]{2,1,0:T(8,128)} %pad_maximum_fusion.5), channel_id=1, source_target_pairs={{0,8},{4,20},{8,0},{12,28},{16,24},{20,4},{24,16},{28,12},{1,9},{5... | collective-permute-start | bytes 3538952 | tf_op jit(solution)/shard_map/ppermute | solution.py:643
  105.5 21.0 %copy-start.4 = (f32[2,192,768]{2,1,0:T(8,128)}, f32[2,192,768]{2,1,0:T(8,128)S(1)}, u32[]{:S(2)}) copy-start(f32[2,192,768]{2,1,0:T(8,128)S(1)} %collective-permute-done.3) | copy-start | bytes 3538948
  105.6 21.0 %collective-permute-start.16 = (f32[1,192,768]{2,1,0:T(8,128)}, f32[1,192,768]{2,1,0:T(8,128)}, u32[]{:S(2)}, u32[]{:S(2)}) collective-permute-start(f32[1,192,768]{2,1,0:T(8,128)} %bitcast.25), channel_id=1, source_target_pairs={{0,16},{4,12},{8,24},{12,4},{16,0},{20,28},{24,8},{28,20},{1,17},{... | collective-permute-start | bytes 1769480 | tf_op jit(solution)/shard_map/ppermute | solution.py:643
  107.8 18.7 %collective-permute-start.15 = (f32[1,192,768]{2,1,0:T(8,128)}, f32[1,192,768]{2,1,0:T(8,128)}, u32[]{:S(2)}, u32[]{:S(2)}) collective-permute-start(f32[1,192,768]{2,1,0:T(8,128)} %bitcast.25), channel_id=1, source_target_pairs={{0,8},{4,20},{8,0},{12,28},{16,24},{20,4},{24,16},{28,12},{1,9},{5... | collective-permute-start | bytes 1769480 | tf_op jit(solution)/shard_map/ppermute | solution.py:643
  127.8 3.5 copy-start.2
  127.8 3.4 copy-start.5
  127.8 24.0 %collective-permute-start.17 = (f32[3,192,768]{2,1,0:T(8,128)S(1)}, f32[3,192,768]{2,1,0:T(8,128)}, u32[]{:S(2)}, u32[]{:S(2)}) collective-permute-start(f32[3,192,768]{2,1,0:T(8,128)S(1)} %pad_maximum_fusion.r_20_), channel_id=1, source_target_pairs={{0,16},{4,12},{8,24},{12,4},{16,0},{20,28},{24,8},{28,20},{1,17},{... | collective-permute-start | bytes 5308424 | tf_op jit(solution)/shard_map/ppermute | solution.py:646
  131.2 22.6 %collective-permute-start.18 = (f32[3,192,768]{2,1,0:T(8,128)}, f32[3,192,768]{2,1,0:T(8,128)}, u32[]{:S(2)}, u32[]{:S(2)}) collective-permute-start(f32[3,192,768]{2,1,0:T(8,128)} %pad_maximum_fusion.1.r_19_), channel_id=1, source_target_pairs={{0,4},{4,0},{8,12},{12,8},{16,20},{20,16},{24,28},{28,24},{1,5},{5... | collective-permute-start | bytes 5308424 | tf_op jit(solution)/shard_map/ppermute | solution.py:649
  131.3 22.5 %collective-permute-start.19 = (f32[3,192,768]{2,1,0:T(8,128)S(1)}, f32[3,192,768]{2,1,0:T(8,128)}, u32[]{:S(2)}, u32[]{:S(2)}) collective-permute-start(f32[3,192,768]{2,1,0:T(8,128)S(1)} %pad_maximum_fusion.r_20_), channel_id=1, source_target_pairs={{0,4},{4,0},{8,12},{12,8},{16,20},{20,16},{24,28},{28,24},{1,5},{5... | collective-permute-start | bytes 5308424 | tf_op jit(solution)/shard_map/ppermute | solution.py:649
  134.2 18.2 %copy-start.11 = (bf16[2,768]{1,0:T(2,128)(2,1)S(1)}, bf16[2,768]{1,0:T(2,128)(2,1)}, u32[]{:S(2)}) copy-start(bf16[2,768]{1,0:T(2,128)(2,1)} %param.25) | copy-start | bytes 9220
  134.2 18.2 %copy-start.12 = (bf16[2,768]{1,0:T(2,128)(2,1)S(1)}, bf16[2,768]{1,0:T(2,128)(2,1)}, u32[]{:S(2)}) copy-start(bf16[2,768]{1,0:T(2,128)(2,1)} %param.24) | copy-start | bytes 9220
  134.2 18.2 %copy-start.13 = (bf16[2,768]{1,0:T(2,128)(2,1)S(1)}, bf16[2,768]{1,0:T(2,128)(2,1)}, u32[]{:S(2)}) copy-start(bf16[2,768]{1,0:T(2,128)(2,1)} %param.23) | copy-start | bytes 9220
  134.2 18.9 %slice-start = ((f32[104,768]{1,0:T(8,128)}), f32[1,768]{1,0:T(1,128)S(1)}, s32[]{:S(2)}) async-start(f32[104,768]{1,0:T(8,128)} %copy-done.7), calls=%async_computation | async-start | bytes 6144 | tf_op jit(solution)/shard_map/slice | solution.py:774
  134.2 18.9 %slice-start.1 = ((f32[104,768]{1,0:T(8,128)}), f32[1,768]{1,0:T(1,128)S(1)}, s32[]{:S(2)}) async-start(f32[104,768]{1,0:T(8,128)} %copy-done.8), calls=%async_computation.1 | async-start | bytes 6144 | tf_op jit(solution)/shard_map/slice | solution.py:774
  134.3 18.9 %slice-start.2 = ((f32[104,768]{1,0:T(8,128)}), f32[1,768]{1,0:T(1,128)S(1)}, s32[]{:S(2)}) async-start(f32[104,768]{1,0:T(8,128)} %copy-done.9), calls=%async_computation.2 | async-start | bytes 6144 | tf_op jit(solution)/shard_map/slice | solution.py:774
  134.3 19.5 %collective-permute-start.20 = (f32[3,192,768]{2,1,0:T(8,128)}, f32[3,192,768]{2,1,0:T(8,128)}, u32[]{:S(2)}, u32[]{:S(2)}) collective-permute-start(f32[3,192,768]{2,1,0:T(8,128)} %pad_maximum_fusion.2.r_21_), channel_id=1, source_target_pairs={{0,4},{4,0},{8,12},{12,8},{16,20},{20,16},{24,28},{28,24},{1,5},{5... | collective-permute-start | bytes 5308424 | tf_op jit(solution)/shard_map/ppermute | solution.py:649
  151.8 4.2 %collective-permute-start.21 = (f32[3,192,768]{2,1,0:T(8,128)}, f32[3,192,768]{2,1,0:T(8,128)}, u32[]{:S(2)}, u32[]{:S(2)}) collective-permute-start(f32[3,192,768]{2,1,0:T(8,128)} %collective-permute-done.17.r_22_), channel_id=1, source_target_pairs={{0,4},{4,0},{8,12},{12,8},{16,20},{20,16},{24,28},{28,24},{1,5},{5... | collective-permute-start | bytes 5308424 | tf_op jit(solution)/shard_map/ppermute | solution.py:649
  245.0 25.6 %collective-permute-start.22 = (f32[1,4,96,1920]{3,2,1,0:T(8,128)}, f32[1,4,96,1920]{3,2,1,0:T(8,128)S(1)}, u32[]{:S(2)}, u32[]{:S(2)}) collective-permute-start(f32[1,4,96,1920]{3,2,1,0:T(8,128)} %dynamic-slice_bitcast_fusion), channel_id=1, source_target_pairs={{0,4},{4,0},{8,12},{12,8},{16,20},{20,16},{24,28},{28,24},{1,5},{5... | collective-permute-start | bytes 8847368 | tf_op jit(solution)/shard_map/ppermute | solution.py:649
  270.5 35.9 %collective-permute-start.24 = (f32[1,4,96,768]{3,2,1,0:T(8,128)}, f32[1,4,96,768]{3,2,1,0:T(8,128)}, u32[]{:S(2)}, u32[]{:S(2)}) collective-permute-start(f32[1,4,96,768]{3,2,1,0:T(8,128)} %dynamic-slice_bitcast_fusion.1), channel_id=1, source_target_pairs={{0,4},{4,0},{8,12},{12,8},{16,20},{20,16},{24,28},{28,24},{1,5},{5... | collective-permute-start | bytes 3538952 | tf_op jit(solution)/shard_map/ppermute | solution.py:649
  274.2 32.1 %collective-permute-start.23 = (f32[1,2,96,1920]{3,2,1,0:T(8,128)}, f32[1,2,96,1920]{3,2,1,0:T(8,128)}, u32[]{:S(2)}, u32[]{:S(2)}) collective-permute-start(f32[1,2,96,1920]{3,2,1,0:T(8,128)} %pad_maximum_fusion.4), channel_id=1, source_target_pairs={{0,8},{4,20},{8,0},{12,28},{16,24},{20,4},{24,16},{28,12},{1,9},{5... | collective-permute-start | bytes 4423688 | tf_op jit(solution)/shard_map/ppermute | solution.py:668
  274.7 31.7 %copy-start.1 = (f32[8,96,768]{2,1,0:T(8,128)S(1)}, f32[8,96,768]{2,1,0:T(8,128)}, u32[]{:S(2)}) copy-start(f32[8,96,768]{2,1,0:T(8,128)} %dynamic_update_slice.3) | copy-start | bytes 7077892
  308.8 35.8 %collective-permute-start.26 = (f32[1,2,96,768]{3,2,1,0:T(8,128)}, f32[1,2,96,768]{3,2,1,0:T(8,128)S(1)}, u32[]{:S(2)}, u32[]{:S(2)}) collective-permute-start(f32[1,2,96,768]{3,2,1,0:T(8,128)} %pad_maximum_fusion.7), channel_id=1, source_target_pairs={{0,8},{4,20},{8,0},{12,28},{16,24},{20,4},{24,16},{28,12},{1,9},{5... | collective-permute-start | bytes 1769480 | tf_op jit(solution)/shard_map/ppermute | solution.py:668
  312.0 32.5 %collective-permute-start.25 = (f32[1,96,1920]{2,1,0:T(8,128)S(1)}, f32[1,96,1920]{2,1,0:T(8,128)}, u32[]{:S(2)}, u32[]{:S(2)}) collective-permute-start(f32[1,96,1920]{2,1,0:T(8,128)S(1)} %dynamic-slice_bitcast_fusion.2), channel_id=1, source_target_pairs={{0,16},{4,12},{8,24},{12,4},{16,0},{20,28},{24,8},{28,20},{1,17},{... | collective-permute-start | bytes 2211848 | tf_op jit(solution)/shard_map/ppermute | solution.py:675
  345.9 6.8 %collective-permute-start.27 = (f32[1,96,768]{2,1,0:T(8,128)S(1)}, f32[1,96,768]{2,1,0:T(8,128)S(1)}, u32[]{:S(2)}, u32[]{:S(2)}) collective-permute-start(f32[1,96,768]{2,1,0:T(8,128)S(1)} %dynamic-slice_bitcast_fusion.3), channel_id=1, source_target_pairs={{0,16},{4,12},{8,24},{12,4},{16,0},{20,28},{24,8},{28,20},{1,17},{... | collective-permute-start | bytes 884744 | tf_op jit(solution)/shard_map/ppermute | solution.py:675

commit v2 on v1

--- a/solution.py
+++ b/solution.py
@@ -240,7 +240,9 @@
         one(0, blk)
 
 
-def bwd_own_kernel(xs_ref, xl_ref, p_ref, o_ref, do_ref, dp_ref, gw_ref, gb_ref, **kw):
+def bwd_own_kernel(
+    xs_ref, xl_ref, p_ref, o_ref, do_ref, dp_ref, gw_ref, gb_ref, *, n_dp, **kw
+):
     b = pl.program_id(0)
     long0 = kw["nshort"] * kw["short_slot"] // kw["blk"]
 
@@ -263,6 +265,28 @@
         gw_ref[...] += dot(xl_ref[...], dp_ref[...], TN)
 
     gb_ref[...] += jnp.sum(dp_ref[...].astype(F32).reshape(-1, 8, 768), axis=0)
+
+    @pl.when(b == pl.num_programs(0) - 1)
+    def _():
+        d, heads = gw_ref.shape[0], kw["heads"]
+        hw, r, part = heads * HD, d // n_dp, HD // n_dp
+        total = jnp.sum(gb_ref[...], axis=0, keepdims=True)
+        row = lax.broadcasted_iota(jnp.int32, (d, 1), 0)
+        owner = sum((row >= i * r).astype(jnp.int32) for i in range(1, n_dp))
+        k = row - owner * r
+        h = sum((k >= i * part).astype(jnp.int32) for i in range(1, heads + 1))
+        n = jnp.where(h < heads, h * HD + owner * part + k - h * part, -1)
+        lane = lax.broadcasted_iota(jnp.int32, (1, 256), 1)
+        spare = lane[:, 128:]
+
+        def column(v):
+            return jnp.sum(jnp.where(lane == n, v, 0.0), axis=1, keepdims=True)
+
+        gw_ref[:, 128:256] += jnp.where(
+            spare == hw,
+            column(total[:, 0:256]),
+            jnp.where(spare == hw + 1, column(total[:, 512:768]), 0.0),
+        )
 
 
 def bwd_own(xs, xl, p, o, do, blk, **kw):
@@ -279,13 +303,12 @@
         out_specs=[
             pl.BlockSpec((blk, 768), lambda b: (b, 0)),
             pl.BlockSpec((d, 768), lambda b: (0, 0)),
-            pl.BlockSpec((8, 768), lambda b: (0, 0)),
         ],
         out_shape=[
             jax.ShapeDtypeStruct((rows, 768), BF),
             jax.ShapeDtypeStruct((d, 768), F32),
-            jax.ShapeDtypeStruct((8, 768), F32),
         ],
+        scratch_shapes=[pltpu.VMEM((8, 768), F32)],
         compiler_params=pltpu.CompilerParams(vmem_limit_bytes=60 * 2**20),
         cost_estimate=pl.CostEstimate(flops=18 * 10**9, bytes_accessed=2**23, transcendentals=0),
         name="attn_bwd_own",
@@ -459,19 +482,26 @@
 
             return put
 
-        def store_out(n):
-            def put(at):
-                row = place_ref[2, n]
-
-                @pl.when(row >= 0)
-                def _():
-                    @pl.loop(0, slots - 1)
-                    def _(j):
-                        wo_s[j + 1, pl.ds(pl.multiple_of(row, 32), r)] = stage[at, j].astype(BF)
-
-            return put
-
-        jobs = [(w1_pieces[n], None, store_out(n)) for n in range(8)]
+        def out_rows(n, do):
+            row = place_ref[2, n]
+
+            @pl.when(row >= 0)
+            def _():
+                at = row // r
+                do(pltpu.make_async_copy(w1_pieces[n], stage.at[at], sems.at[at]), at, row)
+
+        def store_out(copy, at, row):
+            copy.wait()
+
+            @pl.loop(0, slots - 1)
+            def _(j):
+                wo_s[j + 1, pl.ds(pl.multiple_of(row, 32), r)] = stage[at, j].astype(BF)
+
+        for n in range(8):
+            out_rows(n, lambda copy, at, row: copy.start())
+        for n in range(8):
+            out_rows(n, store_out)
+        jobs = []
         for n in range(8):
             jobs.append((w2_pieces[n].at[:, pl.ds(0, r)], None, store(wu_s, n)))
             jobs.append((w2_pieces[n].at[:, pl.ds(r, r)], None, store(wd_s, n)))
@@ -556,6 +586,7 @@
     slots = o.shape[0]
     fl = own[1].shape[1]
     r = pieces[0].shape[1]
+    assert hw <= 4 * r
     long0 = srows // blk
     row = lambda i, *_: (i, 0)
     grp = lambda i, *_: (0, i, 0)
@@ -627,11 +658,9 @@
         at = (self.low * extra + lax.axis_index("dp") // 8) * r
         return lax.dynamic_slice_in_dim(shard, at, r, 0).astype(F32)
 
-    def along_tensor(self, piece):
+    def along_tensor(self, piece, shift):
         n = self.n_tensor
-        return [
-            lax.ppermute(piece, "tensor", [(i, (i + s) % n) for i in range(n)]) for s in range(1, n)
-        ]
+        return lax.ppermute(piece, "tensor", [(i, (i + shift) % n) for i in range(n)])
 
     def whole_eighth(self, z):
         if self.n_dp == 8:
@@ -721,7 +750,9 @@
         small = jnp.concatenate([small, jnp.zeros((6, d), F32)], 0)
         piece = wires.piece(w1_own)
         pr = piece.shape[0]
-        z = wires.along_tensor(jnp.concatenate([small, piece], 0))
+        piece = jnp.concatenate([small, piece], 0)
+        near = [wires.along_tensor(piece, s) for s in (1, n_tensor - 1)]
+        far = wires.along_tensor(after(*near), 1)
         row = wires.source * r
         c = row // hw
         place = jnp.stack(
@@ -740,18 +771,27 @@
         xs, xl = short_tokens.reshape(srows, d), long_tokens.reshape(-1, d)
         cs, cl = short_cotangent.reshape(srows, d), long_cotangent.reshape(-1, d)
         lens = jnp.concatenate([short_lengths, long_lengths])
-        po = attn_fwd(0, lens, place, xs, xl, w1_own, bias_of(small), None, slots=n_tensor, **kw)
-
-        t1 = wires.whole_eighth(after(jnp.stack([x[8:] for x in z]), po[1]))
-        a1, b1 = wires.first_hop(t1)
-        piece2 = after(jnp.stack([wires.piece(w_up), wires.piece(w_down)]), po[1])
-        z2 = wires.along_tensor(piece2)
-        c1 = wires.second_hop(after(a1, z2[0]))
-        w1 = [t1, a1, b1, c1]
-        w1 += [wires.to_pair(x) for x in w1[:3]] + [wires.to_pair(after(c1, z2[2]))]
         def eighths(*x):
             return wires.whole_eighth(jnp.stack(x)).reshape(len(x), -1, d)
 
+        def join(u, v):
+            return jnp.concatenate([u[:1], v, u[1:]], 0)
+
+        t1 = eighths(*[x[8:] for x in near])
+        a1, b1 = wires.first_hop(t1)
+        bias = after(bias_of(small), *near)
+        po = attn_fwd(0, lens, place, xs, xl, w1_own, bias, None, slots=n_tensor, **kw)
+        a1, b1, far, *po = lax.optimization_barrier((a1, b1, far, *po))
+        z = [near[0], far, near[1]]
+        t1b = eighths(far[8:])
+        a1b, b1b = wires.first_hop(t1b)
+        piece2 = after(jnp.stack([wires.piece(w_up), wires.piece(w_down)]), po[1])
+        z2 = [wires.along_tensor(piece2, s) for s in (1, n_tensor - 1)]
+        z2.insert(1, wires.along_tensor(z2[0], 1))
+        a1, b1b, _ = lax.optimization_barrier((join(a1, a1b), b1b, z2[0]))
+        c1 = wires.second_hop(a1)
+        w1 = [join(t1, t1b), a1, join(b1, b1b), c1]
+        w1 += [wires.to_pair(x) for x in w1[:3]] + [wires.to_pair(after(c1, z2[2]))]
         t2 = eighths(z2[0], z2[2])
         a2, b2 = wires.first_hop(t2)
         for s in range(1, n_tensor):
@@ -762,10 +802,7 @@
                 a2b, b2b = wires.first_hop(t2b)
             if s == 2:
                 a2b, b2b, *po = lax.optimization_barrier((a2b, b2b, *po))
-                t2, a2, b2 = [
-                    jnp.concatenate([u[:1], v, u[1:]], 0)
-                    for u, v in ((t2, t2b), (a2, a2b), (b2, b2b))
-                ]
+                t2, a2, b2 = join(t2, t2b), join(a2, a2b), join(b2, b2b)
                 c2 = wires.second_hop(a2)
         c2, *po = lax.optimization_barrier((c2, *po))
         w2 = [t2, a2, b2, c2]
@@ -779,14 +816,10 @@
         fl = w_up.shape[1]
         gall = wires.split(gall)
         got = wires.halve_pair(gall)
-        dp_own, gw, gb = bwd_own(xs, xl, p, o, do, **kw)
+        dp_own, gw = bwd_own(xs, xl, p, o, do, n_dp=n_dp, **kw)
         gall = wires.sum_pair(gall, after(got, dp_own))
         got = wires.halve_first(gall)
-        gb = gb.sum(0).reshape(3, 256)
-        gb = jnp.stack([gb[0, :hw], gb[2, :hw]]).reshape(2 * heads, n_dp, hd // n_dp)
-        gb = gb.transpose(1, 0, 2).reshape(n_dp, 1, -1)
-        gw = lax.dynamic_update_slice(gw.reshape(n_dp, d // n_dp, 768), gb, (0, 0, hw))
-        gw = wires.split(gw.reshape(d, 768))
+        gw = wires.split(gw)
         gotw = wires.halve_pair(gw)
         nb = (ns * ss + nl * ls) // blk
         rest = (place, p, o, do, dp_own, dh, w1_own, w1, srows)
@@ -804,7 +837,8 @@
         gw = wires.sum_second(gw, gotw)
         small_shard = gall[:, 2 * fl + 256 : 2 * fl + 264].T
         gqkv = gw.reshape(-1, 3, 256)[:, :, :hw].transpose(1, 0, 2)
-        qv_shard = gw[0, hw : hw + 2 * hw // n_dp].reshape(2, heads, hd // n_dp)
+        kept = hw // n_dp
+        qv_shard = jnp.stack([gw[:kept, hw], gw[:kept, hw + 1]]).reshape(2, heads, hd // n_dp)
         return (
             es.reshape(ns, ss, d),
             el.reshape(nl, ls, d),

time: 360 us -> 355 us (0.986)
  starting transfers between devices: 30.1 us -> 21.6 us
  waiting for transfers between devices: 44.2 us -> 48.3 us
    ppermute x6, waiting for transfers between devices: 34.4 us -> 28.1 us  [along_tensor(): lax.ppermute(piece, 'tensor', [(i, (i + shift) % n) for i in range(n)])]
    ppermute x3 -> x4, waiting for transfers between devices: 4.71 us -> 10.3 us  [first_hop(): lax.ppermute(z, 'dp', self.second)]
    ppermute x3 -> x4, waiting for transfers between devices: 1.37 us -> 6.25 us  [first_hop(): lax.ppermute(z, 'dp', self.first)]
  transfers between devices with their start and end apart: 28 -> 30, of which waited for: 8 -> 9; matrix products, arithmetic and copies ran while one was open for 9% -> 8% of each run, Pallas kernels for 42% -> 43%
where the time goes in v2:
time: 355 us; the launch traced here: 349 us
  Pallas kernels  234 us (66%)
  waiting for transfers between devices  48.3 us (14%)
  other arithmetic  22.1 us (6%)
  starting transfers between devices  21.6 us (6%)
  local copies, waits for them, and re-layouts  20.3 us (6%)
    pallas_call x1, Pallas kernels, ffn_block(): pl.pallas_call(lambda *r: ffn_kernel(*r, long0=long0, hw=hw), grid_spec=p...  84.3 us
    pallas_call x4, Pallas kernels, attn_fwd(): pl.pallas_call(lambda *r: attn_fwd_kernel(*r, own=slot == 0, nshort=nshor...  67.7 us
    pallas_call x2, Pallas kernels, bwd_rest(): pl.pallas_call(lambda *r: bwd_rest_kernel(*r, lo=lo, blk=blk, **kw), grid...  63.2 us
    ppermute x6, waiting for transfers between devices, along_tensor(): lax.ppermute(piece, 'tensor', [(i, (i + shift) % n) for i in range(n)])  28.1 us
    pallas_call x1, Pallas kernels, bwd_own(): pl.pallas_call(lambda *r: bwd_own_kernel(*r, blk=blk, **kw), grid=(rows /...  19.3 us
    ppermute x4, waiting for transfers between devices, first_hop(): lax.ppermute(z, 'dp', self.second)  10.3 us
    ppermute x6, starting transfers between devices, along_tensor(): lax.ppermute(piece, 'tensor', [(i, (i + shift) % n) for i in range(n)])  7.4 us
  transfers between devices with their start and end apart: 30, of which 9 were waited for; matrix products, arithmetic and copies ran while one was open for 8% of the time, Pallas kernels for 43%

profile of v2, /device:TPU:0, one launch (start us, length us, event | category | flops | bytes accessed | tf_op | source)
XLA Modules:
  0.0 348.6 jit_solution(3566451984826692183)
XLA Ops:
  1.4 0.7 convert_element_type.16
  2.3 1.1 fusion.2
  3.4 5.1 %collective-permute-start.1 = (f32[104,768]{1,0:T(8,128)S(1)}, f32[104,768]{1,0:T(8,128)S(1)}, u32[]{:S(2)}, u32[]{:S(2)}) collective-permute-start(f32[104,768]{1,0:T(8,128)S(1)} %pad_maximum_fusion.11), channel_id=1, source_target_pairs={{0,3},{1,0},{2,1},{3,2},{4,7},{5,4},{6,5},{7,6},{8,11},{9,8},{10,9... | collective-permute-start | bytes 958472 | tf_op jit(solution)/shard_map/ppermute | solution.py:663
  9.5 1.0 dynamic-slice_bitcast_fusion.4
  11.1 1.1 pad_maximum_fusion.3.r_6_.r_8_
  12.9 3.6 %collective-permute-done.1 = f32[104,768]{1,0:T(8,128)S(1)} collective-permute-done((f32[104,768]{1,0:T(8,128)S(1)}, f32[104,768]{1,0:T(8,128)S(1)}, u32[]{:S(2)}, u32[]{:S(2)}) %collective-permute-start.1) | collective-permute-done | bytes 319520 | tf_op jit(solution)/shard_map/ppermute | solution.py:663
  16.5 6.6 %collective-permute-done = f32[104,768]{1,0:T(8,128)S(1)} collective-permute-done((f32[104,768]{1,0:T(8,128)S(1)}, f32[104,768]{1,0:T(8,128)S(1)}, u32[]{:S(2)}, u32[]{:S(2)}) %collective-permute-start) | collective-permute-done | bytes 319520 | tf_op jit(solution)/shard_map/ppermute | solution.py:663
  23.2 1.6 collective-permute-start.3
  24.8 1.5 collective-permute-start.2
  26.3 1.6 collective-permute-start.4
  27.9 16.0 %attn_fwd.4 = (bf16[4,2048,768]{2,1,0:T(8,128)(2,1)}, bf16[4,2048,256]{2,1,0:T(8,128)(2,1)}) custom-call(s32[5]{0:T(128)} %pad_add_fusion.1.r_0_, s32[3,8]{1,0:T(4,128)} %pad_add_fusion.r_1_.r_0_, s32[1]{0:T(128)} %constant.97.clone.1.r_2_, bf16[512,768]{1,0:T(8,128)(2,1)} %bitcast.105, bf16[1536,768]{1,0:T(8,128)(2,1)} %bitcast.98, ...), custom_call_target="tpu_custom_call" | custom-call | flops 14000000000 | bytes 8388608 | tf_op jit(solution)/shard_map/attn_fwd/pallas_call | solution.py:164
  45.1 6.2 %collective-permute-done.10 = f32[1,96,768]{2,1,0:T(8,128)S(1)} collective-permute-done((f32[1,96,768]{2,1,0:T(8,128)S(1)}, f32[1,96,768]{2,1,0:T(8,128)S(1)}, u32[]{:S(2)}, u32[]{:S(2)}) %collective-permute-start.10) | collective-permute-done | bytes 294944 | tf_op jit(solution)/shard_map/ppermute | solution.py:672
  51.4 1.0 pad_maximum_fusion.7.r_7_.r_12_.r_8_
  52.4 8.0 %collective-permute-done.5 = f32[2,96,768]{2,1,0:T(8,128)S(1)} collective-permute-done((f32[2,96,768]{2,1,0:T(8,128)S(1)}, f32[2,96,768]{2,1,0:T(8,128)S(1)}, u32[]{:S(2)}, u32[]{:S(2)}) %collective-permute-start.5) | collective-permute-done | bytes 589856 | tf_op jit(solution)/shard_map/ppermute | solution.py:663
  61.7 1.0 pad_maximum_fusion.8.r_8_.r_13_.r_9_
  62.7 9.8 %collective-permute-done.6 = f32[2,96,768]{2,1,0:T(8,128)S(1)} collective-permute-done((f32[2,96,768]{2,1,0:T(8,128)S(1)}, f32[2,96,768]{2,1,0:T(8,128)S(1)}, u32[]{:S(2)}, u32[]{:S(2)}) %collective-permute-start.6) | collective-permute-done | bytes 589856 | tf_op jit(solution)/shard_map/ppermute | solution.py:663
  72.5 1.3 collective-permute-done.12.r_9_.r_14_.r_10_
  74.5 0.8 fusion.9
  76.0 0.8 fusion.8
  77.5 1.1 pad_maximum_fusion.5
  79.8 17.2 %attn_fwd.5 = (bf16[4,2048,768]{2,1,0:T(8,128)(2,1)}, bf16[4,2048,256]{2,1,0:T(8,128)(2,1)}) custom-call(s32[5]{0:T(128)} %pad_add_fusion.1.r_0_, s32[3,8]{1,0:T(4,128)} %pad_add_fusion.r_1_.r_0_, s32[1]{0:T(128)} %constant.98.clone.1.r_2_, bf16[512,768]{1,0:T(8,128)(2,1)} %bitcast.106, ...), custom_call_target="tpu_custom_call", output_to_operand_aliasing={{0}: (14, {}), {1}: (15, {})} | custom-call | flops 14000000000 | bytes 8388608 | tf_op jit(solution)/shard_map/attn_fwd/pallas_call | solution.py:164
  97.0 10.3 %collective-permute-done.8 = f32[2,192,768]{2,1,0:T(8,128)S(1)} collective-permute-done((f32[2,192,768]{2,1,0:T(8,128)}, f32[2,192,768]{2,1,0:T(8,128)S(1)}, u32[]{:S(2)}, u32[]{:S(2)}) %collective-permute-start.8) | collective-permute-done | bytes 1179680 | tf_op jit(solution)/shard_map/ppermute | solution.py:672
  108.0 17.1 %attn_fwd.6 = (bf16[4,2048,768]{2,1,0:T(8,128)(2,1)}, bf16[4,2048,256]{2,1,0:T(8,128)(2,1)}) custom-call(s32[5]{0:T(128)} %pad_add_fusion.1.r_0_, s32[3,8]{1,0:T(4,128)} %pad_add_fusion.r_1_.r_0_, s32[1]{0:T(128)} %constant.99.clone.1.r_2_, bf16[512,768]{1,0:T(8,128)(2,1)} %bitcast.107, ...), custom_call_target="tpu_custom_call", output_to_operand_aliasing={{0}: (14, {}), {1}: (15, {})} | custom-call | flops 14000000000 | bytes 8388608 | tf_op jit(solution)/shard_map/attn_fwd/pallas_call | solution.py:164
  125.3 1.2 pad_maximum_fusion.r_20_
  126.5 1.6 collective-permute-start.19
  128.1 1.3 pad_maximum_fusion.1.r_19_
  130.1 2.4 pad_maximum_fusion.2.r_21_
  132.6 17.4 %attn_fwd.7 = (bf16[4,2048,768]{2,1,0:T(8,128)(2,1)}, bf16[4,2048,256]{2,1,0:T(8,128)(2,1)}) custom-call(s32[5]{0:T(128)} %pad_add_fusion.1.r_0_, s32[3,8]{1,0:T(4,128)} %pad_add_fusion.r_1_.r_0_, s32[1]{0:T(128)} %constant.100.clone.1.r_2_, bf16[512,768]{1,0:T(8,128)(2,1)} %bitcast.108, ...), custom_call_target="tpu_custom_call", output_to_operand_aliasing={{0}: (14, {}), {1}: (15, {})} | custom-call | flops 14000000000 | bytes 8388608 | tf_op jit(solution)/shard_map/attn_fwd/pallas_call | solution.py:164
  151.3 0.7 slice.144
  152.7 1.5 collective-permute-done.23.r_26_
  154.2 84.3 %ffn_block.1 = (bf16[512,768]{1,0:T(8,128)(2,1)}, bf16[1536,768]{1,0:T(8,128)(2,1)}, f32[2048,768]{1,0:T(8,128)}, bf16[4,2048,256]{2,1,0:T(8,128)(2,1)}, f32[768,1920]{1,0:T(8,128)}) custom-call(s32[3,8]{1,0:T(4,128)} %pad_add_fusion.r_1_.r_0_, bf16[512,768]{1,0:T(8,128)(2,1)} %bitcast.109, bf16[1536,768]{1,0:T(8,128)(2,1)} %bitcast.102, ...), custom_call_target="tpu_custom_call" | custom-call | flops 80000000000 | bytes 33554432 | tf_op jit(solution)/shard_map/ffn_block/pallas_call | solution.py:594
  238.5 3.6 %dynamic-slice_bitcast_fusion = f32[1,4,96,1920]{3,2,1,0:T(8,128)} fusion(f32[1,4,2,96,1920]{4,3,2,1,0:T(8,128)} %bitcast.75, s32[]{:T(128)S(6)} %select_n.114), kind=kLoop, calls=%fused_computation.1 | loop fusion | bytes 5898244 | tf_op jit(solution)/shard_map/jit(dynamic_index_in_dim)/squeeze | solution.py:686
  242.5 19.3 %attn_bwd_own.1 = (bf16[2048,768]{1,0:T(8,128)(2,1)}, f32[768,768]{1,0:T(8,128)}) custom-call(bf16[512,768]{1,0:T(8,128)(2,1)} %bitcast.110, bf16[1536,768]{1,0:T(8,128)(2,1)} %bitcast.103, bf16[4,2048,768]{2,1,0:T(8,128)(2,1)} %get-tuple-element.92.r_2_.r_1_, bf16[4,2048,256]{2,1,0:T(8,128)(2,1)} %get-tuple-element.86.r_5_.r_3_.r_2_, ...), custom_call_target="tpu_custom_call" | custom-call | flops 17999998976 | bytes 8388608 | tf_op jit(solution)/shard_map/attn_bwd_own/pallas_call | solution.py:294
  261.9 2.4 dynamic-slice_bitcast_fusion.1
  264.4 2.1 bitcast_add_fusion
  266.8 1.3 pad_maximum_fusion.4
  268.0 1.8 collective-permute-start.25
  269.8 31.7 %attn_bwd_rest.2 = (f32[512,768]{1,0:T(8,128)}, f32[1536,768]{1,0:T(8,128)}) custom-call(s32[3,8]{1,0:T(4,128)} %pad_add_fusion.r_1_.r_0_, bf16[4,2048,768]{2,1,0:T(8,128)(2,1)} %get-tuple-element.92.r_2_.r_1_, bf16[4,2048,256]{2,1,0:T(8,128)(2,1)} %get-tuple-element.86.r_5_.r_3_.r_2_, bf16[4,2048,256]{2,1,0:T(8,128)(2,1)} %get-tuple-element.93.r_4_.r_3_, ...), custom_call_target="tpu_custom_call" | custom-call | flops 24999999488 | bytes 8388608 | tf_op jit(solution)/shard_map/attn_bwd_rest/pallas_call | solution.py:395
  301.6 1.4 bitcast_add_fusion.1
  303.1 0.9 pad_maximum_fusion.10
  304.3 1.5 maximum_add_fusion
  306.5 31.4 %attn_bwd_rest.3 = f32[1536,768]{1,0:T(8,128)} custom-call(s32[3,8]{1,0:T(4,128)} %pad_add_fusion.r_1_.r_0_, bf16[4,2048,768]{2,1,0:T(8,128)(2,1)} %get-tuple-element.92.r_2_.r_1_, bf16[4,2048,256]{2,1,0:T(8,128)(2,1)} %get-tuple-element.86.r_5_.r_3_.r_2_, bf16[4,2048,256]{2,1,0:T(8,128)(2,1)} %get-tuple-element.93.r_4_.r_3_, ...), custom_call_target="tpu_custom_call", output_to_operand_aliasing={{}: (15, {})} | custom-call | flops 24999999488 | bytes 8388608 | tf_op jit(solution)/shard_map/attn_bwd_rest/pallas_call | solution.py:395
  337.9 1.2 fusion
  339.3 1.7 collective-permute-start.29
  341.7 0.7 copy.58
  344.4 0.8 slice_bitcast_fusion.1
  345.2 0.9 collective-permute-done.29
  347.3 0.8 copy.56
  (145 shorter events, 18.2 us)
Async XLA Ops:
  0.6 8.1 %copy-start.11 = (f32[64]{0:T(128)S(1)}, f32[64]{0:T(128)}, u32[]{:S(2)}) copy-start(f32[64]{0:T(128)} %constant.101.clone) | copy-start | bytes 772
  2.1 8.4 %copy-start.12 = (f32[1,768]{1,0:T(1,128)}, f32[1,768]{1,0:T(1,128)S(1)}, u32[]{:S(2)}) copy-start(f32[1,768]{1,0:T(1,128)S(1)} %convert_element_type.16) | copy-start | bytes 9220
  2.2 8.9 %copy-start = (bf16[3,768,192]{1,2,0:T(8,128)(2,1)S(1)}, bf16[3,768,192]{1,2,0:T(8,128)(2,1)}, u32[]{:S(2)}) copy-start(bf16[3,768,192]{1,2,0:T(8,128)(2,1)} %param.20) | copy-start | bytes 2654212
  2.3 8.9 %copy-start.3 = (bf16[192,768]{1,0:T(8,128)(2,1)S(1)}, bf16[192,768]{1,0:T(8,128)(2,1)}, u32[]{:S(2)}) copy-start(bf16[192,768]{1,0:T(8,128)(2,1)} %param.22) | copy-start | bytes 884740
  3.4 13.1 %collective-permute-start.1 = (f32[104,768]{1,0:T(8,128)S(1)}, f32[104,768]{1,0:T(8,128)S(1)}, u32[]{:S(2)}, u32[]{:S(2)}) collective-permute-start(f32[104,768]{1,0:T(8,128)S(1)} %pad_maximum_fusion.11), channel_id=1, source_target_pairs={{0,3},{1,0},{2,1},{3,2},{4,7},{5,4},{6,5},{7,6},{8,11},{9,8},{10,9... | collective-permute-start | bytes 958472 | tf_op jit(solution)/shard_map/ppermute | solution.py:663
  8.6 14.5 %collective-permute-start = (f32[104,768]{1,0:T(8,128)S(1)}, f32[104,768]{1,0:T(8,128)S(1)}, u32[]{:S(2)}, u32[]{:S(2)}) collective-permute-start(f32[104,768]{1,0:T(8,128)S(1)} %pad_maximum_fusion.11), channel_id=1, source_target_pairs={{0,1},{1,2},{2,3},{3,0},{4,5},{5,6},{6,7},{7,4},{8,9},{9,10},{10,1... | collective-permute-start | bytes 958472 | tf_op jit(solution)/shard_map/ppermute | solution.py:663
  16.5 6.6 %copy-start.7 = (f32[104,768]{1,0:T(8,128)}, f32[104,768]{1,0:T(8,128)S(1)}, u32[]{:S(2)}) copy-start(f32[104,768]{1,0:T(8,128)S(1)} %collective-permute-done.1) | copy-start | bytes 958468
  23.1 20.8 %copy-start.9 = (f32[104,768]{1,0:T(8,128)}, f32[104,768]{1,0:T(8,128)S(1)}, u32[]{:S(2)}) copy-start(f32[104,768]{1,0:T(8,128)S(1)} %collective-permute-done) | copy-start | bytes 958468
  23.2 20.7 %collective-permute-start.3 = (f32[2,96,768]{2,1,0:T(8,128)S(1)}, f32[2,96,768]{2,1,0:T(8,128)S(1)}, u32[]{:S(2)}, u32[]{:S(2)}) collective-permute-start(f32[2,96,768]{2,1,0:T(8,128)S(1)} %pad_maximum_fusion.9), channel_id=1, source_target_pairs={{0,16},{4,12},{8,24},{12,4},{16,0},{20,28},{24,8},{28,20},{1,17},{... | collective-permute-start | bytes 1769480 | tf_op jit(solution)/shard_map/ppermute | solution.py:672
  24.8 19.1 %collective-permute-start.2 = (f32[2,96,768]{2,1,0:T(8,128)S(1)}, f32[2,96,768]{2,1,0:T(8,128)S(1)}, u32[]{:S(2)}, u32[]{:S(2)}) collective-permute-start(f32[2,96,768]{2,1,0:T(8,128)S(1)} %pad_maximum_fusion.9), channel_id=1, source_target_pairs={{0,8},{4,20},{8,0},{12,28},{16,24},{20,4},{24,16},{28,12},{1,9},{5... | collective-permute-start | bytes 1769480 | tf_op jit(solution)/shard_map/ppermute | solution.py:672
  26.3 17.6 %collective-permute-start.4 = (f32[104,768]{1,0:T(8,128)S(1)}, f32[104,768]{1,0:T(8,128)S(1)}, u32[]{:S(2)}, u32[]{:S(2)}) collective-permute-start(f32[104,768]{1,0:T(8,128)S(1)} %collective-permute-done), channel_id=1, source_target_pairs={{0,1},{1,2},{2,3},{3,0},{4,5},{5,6},{6,7},{7,4},{8,9},{9,10},{10,1... | collective-permute-start | bytes 958472 | tf_op jit(solution)/shard_map/ppermute | solution.py:663
  43.9 8.5 %copy-start.10 = (f32[104,768]{1,0:T(8,128)}, f32[104,768]{1,0:T(8,128)S(1)}, u32[]{:S(2)}) copy-start(f32[104,768]{1,0:T(8,128)S(1)} %collective-permute-done.4) | copy-start | bytes 958468
  43.9 16.5 %collective-permute-start.5 = (f32[2,96,768]{2,1,0:T(8,128)S(1)}, f32[2,96,768]{2,1,0:T(8,128)S(1)}, u32[]{:S(2)}, u32[]{:S(2)}) collective-permute-start(f32[2,96,768]{2,1,0:T(8,128)S(1)} %maximum_convert_fusion), channel_id=1, source_target_pairs={{0,1},{1,2},{2,3},{3,0},{4,5},{5,6},{6,7},{7,4},{8,9},{9,10},{10,1... | collective-permute-start | bytes 1769480 | tf_op jit(solution)/shard_map/ppermute | solution.py:663
  44.0 7.4 %collective-permute-start.10 = (f32[1,96,768]{2,1,0:T(8,128)S(1)}, f32[1,96,768]{2,1,0:T(8,128)S(1)}, u32[]{:S(2)}, u32[]{:S(2)}) collective-permute-start(f32[1,96,768]{2,1,0:T(8,128)S(1)} %slice_bitcast_fusion.4), channel_id=1, source_target_pairs={{0,8},{4,20},{8,0},{12,28},{16,24},{20,4},{24,16},{28,12},{1,9},{5... | collective-permute-start | bytes 884744 | tf_op jit(solution)/shard_map/ppermute | solution.py:672
  44.6 7.8 %collective-permute-start.11 = (f32[1,96,768]{2,1,0:T(8,128)S(1)}, f32[1,96,768]{2,1,0:T(8,128)S(1)}, u32[]{:S(2)}, u32[]{:S(2)}) collective-permute-start(f32[1,96,768]{2,1,0:T(8,128)S(1)} %slice_bitcast_fusion.4), channel_id=1, source_target_pairs={{0,16},{4,12},{8,24},{12,4},{16,0},{20,28},{24,8},{28,20},{1,17},{... | collective-permute-start | bytes 884744 | tf_op jit(solution)/shard_map/ppermute | solution.py:672
  60.4 13.4 %collective-permute-start.12 = (f32[3,96,768]{2,1,0:T(8,128)}, f32[3,96,768]{2,1,0:T(8,128)}, u32[]{:S(2)}, u32[]{:S(2)}) collective-permute-start(f32[3,96,768]{2,1,0:T(8,128)} %pad_maximum_fusion.7.r_7_.r_12_.r_8_), channel_id=1, source_target_pairs={{0,16},{4,12},{8,24},{12,4},{16,0},{20,28},{24,8},{28,20},{1,17},{... | collective-permute-start | bytes 2654216 | tf_op jit(solution)/shard_map/ppermute | solution.py:675
  60.9 11.6 %collective-permute-start.6 = (f32[2,96,768]{2,1,0:T(8,128)S(1)}, f32[2,96,768]{2,1,0:T(8,128)S(1)}, u32[]{:S(2)}, u32[]{:S(2)}) collective-permute-start(f32[2,96,768]{2,1,0:T(8,128)S(1)} %maximum_convert_fusion), channel_id=1, source_target_pairs={{0,3},{1,0},{2,1},{3,2},{4,7},{5,4},{6,5},{7,6},{8,11},{9,8},{10,9... | collective-permute-start | bytes 1769480 | tf_op jit(solution)/shard_map/ppermute | solution.py:663
  61.0 17.6 %copy-start.6 = (f32[3,96,768]{2,1,0:T(8,128)}, f32[3,96,768]{2,1,0:T(8,128)S(1)}, u32[]{:S(2)}) copy-start(f32[3,96,768]{2,1,0:T(8,128)S(1)} %pad_maximum_fusion.6.r_6_.r_11_.r_7_) | copy-start | bytes 2654212
  61.0 12.8 %copy-start.8 = (f32[104,768]{1,0:T(8,128)S(1)}, f32[104,768]{1,0:T(8,128)}, u32[]{:S(2)}) copy-start(f32[104,768]{1,0:T(8,128)} %copy-done.7) | copy-start | bytes 958468
  61.0 18.1 %collective-permute-start.13 = (f32[3,96,768]{2,1,0:T(8,128)S(1)}, f32[3,96,768]{2,1,0:T(8,128)}, u32[]{:S(2)}, u32[]{:S(2)}) collective-permute-start(f32[3,96,768]{2,1,0:T(8,128)S(1)} %pad_maximum_fusion.6.r_6_.r_11_.r_7_), channel_id=1, source_target_pairs={{0,4},{4,0},{8,12},{12,8},{16,20},{20,16},{24,28},{28,24},{1,5},{5... | collective-permute-start | bytes 2654216 | tf_op jit(solution)/shard_map/ppermute | solution.py:678
  61.1 18.6 %collective-permute-start.14 = (f32[3,96,768]{2,1,0:T(8,128)}, f32[3,96,768]{2,1,0:T(8,128)}, u32[]{:S(2)}, u32[]{:S(2)}) collective-permute-start(f32[3,96,768]{2,1,0:T(8,128)} %pad_maximum_fusion.7.r_7_.r_12_.r_8_), channel_id=1, source_target_pairs={{0,4},{4,0},{8,12},{12,8},{16,20},{20,16},{24,28},{28,24},{1,5},{5... | collective-permute-start | bytes 2654216 | tf_op jit(solution)/shard_map/ppermute | solution.py:678
  62.7 16.4 %collective-permute-start.15 = (f32[3,96,768]{2,1,0:T(8,128)}, f32[3,96,768]{2,1,0:T(8,128)}, u32[]{:S(2)}, u32[]{:S(2)}) collective-permute-start(f32[3,96,768]{2,1,0:T(8,128)} %pad_maximum_fusion.8.r_8_.r_13_.r_9_), channel_id=1, source_target_pairs={{0,4},{4,0},{8,12},{12,8},{16,20},{20,16},{24,28},{28,24},{1,5},{5... | collective-permute-start | bytes 2654216 | tf_op jit(solution)/shard_map/ppermute | solution.py:678
  73.8 6.0 %collective-permute-start.16 = (f32[3,96,768]{2,1,0:T(8,128)}, f32[3,96,768]{2,1,0:T(8,128)}, u32[]{:S(2)}, u32[]{:S(2)}) collective-permute-start(f32[3,96,768]{2,1,0:T(8,128)} %collective-permute-done.12.r_9_.r_14_.r_10_), channel_id=1, source_target_pairs={{0,4},{4,0},{8,12},{12,8},{16,20},{20,16},{24,28},{28,24},{1,5},{5... | collective-permute-start | bytes 2654216 | tf_op jit(solution)/shard_map/ppermute | solution.py:678
  78.6 28.7 %collective-permute-start.8 = (f32[2,192,768]{2,1,0:T(8,128)}, f32[2,192,768]{2,1,0:T(8,128)S(1)}, u32[]{:S(2)}, u32[]{:S(2)}) collective-permute-start(f32[2,192,768]{2,1,0:T(8,128)} %pad_maximum_fusion.5), channel_id=1, source_target_pairs={{0,16},{4,12},{8,24},{12,4},{16,0},{20,28},{24,8},{28,20},{1,17},{... | collective-permute-start | bytes 3538952 | tf_op jit(solution)/shard_map/ppermute | solution.py:672
  79.1 28.2 %collective-permute-start.7 = (f32[2,192,768]{2,1,0:T(8,128)}, f32[2,192,768]{2,1,0:T(8,128)S(1)}, u32[]{:S(2)}, u32[]{:S(2)}) collective-permute-start(f32[2,192,768]{2,1,0:T(8,128)} %pad_maximum_fusion.5), channel_id=1, source_target_pairs={{0,8},{4,20},{8,0},{12,28},{16,24},{20,4},{24,16},{28,12},{1,9},{5... | collective-permute-start | bytes 3538952 | tf_op jit(solution)/shard_map/ppermute | solution.py:672
  79.2 17.8 %collective-permute-start.9 = (f32[2,96,768]{2,1,0:T(8,128)S(1)}, f32[2,96,768]{2,1,0:T(8,128)S(1)}, u32[]{:S(2)}, u32[]{:S(2)}) collective-permute-start(f32[2,96,768]{2,1,0:T(8,128)S(1)} %collective-permute-done.5), channel_id=1, source_target_pairs={{0,1},{1,2},{2,3},{3,0},{4,5},{5,6},{6,7},{7,4},{8,9},{9,10},{10,1... | collective-permute-start | bytes 1769480 | tf_op jit(solution)/shard_map/ppermute | solution.py:663
  107.3 17.9 %copy-start.4 = (f32[2,192,768]{2,1,0:T(8,128)}, f32[2,192,768]{2,1,0:T(8,128)S(1)}, u32[]{:S(2)}) copy-start(f32[2,192,768]{2,1,0:T(8,128)S(1)} %collective-permute-done.8) | copy-start | bytes 3538948
  107.3 18.0 %collective-permute-start.18 = (f32[1,192,768]{2,1,0:T(8,128)S(1)}, f32[1,192,768]{2,1,0:T(8,128)}, u32[]{:S(2)}, u32[]{:S(2)}) collective-permute-start(f32[1,192,768]{2,1,0:T(8,128)S(1)} %bitcast.86), channel_id=1, source_target_pairs={{0,16},{4,12},{8,24},{12,4},{16,0},{20,28},{24,8},{28,20},{1,17},{... | collective-permute-start | bytes 1769480 | tf_op jit(solution)/shard_map/ppermute | solution.py:672
  107.8 17.5 %collective-permute-start.17 = (f32[1,192,768]{2,1,0:T(8,128)S(1)}, f32[1,192,768]{2,1,0:T(8,128)}, u32[]{:S(2)}, u32[]{:S(2)}) collective-permute-start(f32[1,192,768]{2,1,0:T(8,128)S(1)} %bitcast.87), channel_id=1, source_target_pairs={{0,8},{4,20},{8,0},{12,28},{16,24},{20,4},{24,16},{28,12},{1,9},{5... | collective-permute-start | bytes 1769480 | tf_op jit(solution)/shard_map/ppermute | solution.py:672
  126.5 3.0 copy-start.2
  126.5 23.5 %collective-permute-start.19 = (f32[3,192,768]{2,1,0:T(8,128)S(1)}, f32[3,192,768]{2,1,0:T(8,128)}, u32[]{:S(2)}, u32[]{:S(2)}) collective-permute-start(f32[3,192,768]{2,1,0:T(8,128)S(1)} %pad_maximum_fusion.r_20_), channel_id=1, source_target_pairs={{0,16},{4,12},{8,24},{12,4},{16,0},{20,28},{24,8},{28,20},{1,17},{... | collective-permute-start | bytes 5308424 | tf_op jit(solution)/shard_map/ppermute | solution.py:675
  129.4 23.3 %collective-permute-start.20 = (f32[3,192,768]{2,1,0:T(8,128)}, f32[3,192,768]{2,1,0:T(8,128)}, u32[]{:S(2)}, u32[]{:S(2)}) collective-permute-start(f32[3,192,768]{2,1,0:T(8,128)} %pad_maximum_fusion.1.r_19_), channel_id=1, source_target_pairs={{0,4},{4,0},{8,12},{12,8},{16,20},{20,16},{24,28},{28,24},{1,5},{5... | collective-permute-start | bytes 5308424 | tf_op jit(solution)/shard_map/ppermute | solution.py:678
  129.5 23.2 %collective-permute-start.21 = (f32[3,192,768]{2,1,0:T(8,128)S(1)}, f32[3,192,768]{2,1,0:T(8,128)}, u32[]{:S(2)}, u32[]{:S(2)}) collective-permute-start(f32[3,192,768]{2,1,0:T(8,128)S(1)} %pad_maximum_fusion.r_20_), channel_id=1, source_target_pairs={{0,4},{4,0},{8,12},{12,8},{16,20},{20,16},{24,28},{28,24},{1,5},{5... | collective-permute-start | bytes 5308424 | tf_op jit(solution)/shard_map/ppermute | solution.py:678
  132.5 18.1 %copy-start.14 = (bf16[2,768]{1,0:T(2,128)(2,1)S(1)}, bf16[2,768]{1,0:T(2,128)(2,1)}, u32[]{:S(2)}) copy-start(bf16[2,768]{1,0:T(2,128)(2,1)} %param.25) | copy-start | bytes 9220
  132.5 18.1 %copy-start.15 = (bf16[2,768]{1,0:T(2,128)(2,1)S(1)}, bf16[2,768]{1,0:T(2,128)(2,1)}, u32[]{:S(2)}) copy-start(bf16[2,768]{1,0:T(2,128)(2,1)} %param.24) | copy-start | bytes 9220
  132.5 18.1 %copy-start.16 = (bf16[2,768]{1,0:T(2,128)(2,1)S(1)}, bf16[2,768]{1,0:T(2,128)(2,1)}, u32[]{:S(2)}) copy-start(bf16[2,768]{1,0:T(2,128)(2,1)} %param.23) | copy-start | bytes 9220
  132.5 19.6 %slice-start = ((f32[104,768]{1,0:T(8,128)}), f32[1,768]{1,0:T(1,128)S(1)}, s32[]{:S(2)}) async-start(f32[104,768]{1,0:T(8,128)} %copy-done.7), calls=%async_computation | async-start | bytes 6144 | tf_op jit(solution)/shard_map/slice | solution.py:811
  132.5 19.5 %slice-start.1 = ((f32[104,768]{1,0:T(8,128)}), f32[1,768]{1,0:T(1,128)S(1)}, s32[]{:S(2)}) async-start(f32[104,768]{1,0:T(8,128)} %copy-done.10), calls=%async_computation.1 | async-start | bytes 6144 | tf_op jit(solution)/shard_map/slice | solution.py:811
  132.5 19.5 %copy-start.13 = (f32[1,768]{1,0:T(1,128)S(1)}, f32[1,768]{1,0:T(1,128)}, u32[]{:S(2)}) copy-start(f32[1,768]{1,0:T(1,128)} %copy-done.12) | copy-start | bytes 9220
  132.5 20.2 %collective-permute-start.22 = (f32[3,192,768]{2,1,0:T(8,128)}, f32[3,192,768]{2,1,0:T(8,128)}, u32[]{:S(2)}, u32[]{:S(2)}) collective-permute-start(f32[3,192,768]{2,1,0:T(8,128)} %pad_maximum_fusion.2.r_21_), channel_id=1, source_target_pairs={{0,4},{4,0},{8,12},{12,8},{16,20},{20,16},{24,28},{28,24},{1,5},{5... | collective-permute-start | bytes 5308424 | tf_op jit(solution)/shard_map/ppermute | solution.py:678
  150.0 4.2 %collective-permute-start.23 = (f32[3,192,768]{2,1,0:T(8,128)}, f32[3,192,768]{2,1,0:T(8,128)}, u32[]{:S(2)}, u32[]{:S(2)}) collective-permute-start(f32[3,192,768]{2,1,0:T(8,128)} %collective-permute-done.19.r_22_), channel_id=1, source_target_pairs={{0,4},{4,0},{8,12},{12,8},{16,20},{20,16},{24,28},{28,24},{1,5},{5... | collective-permute-start | bytes 5308424 | tf_op jit(solution)/shard_map/ppermute | solution.py:678
  242.2 22.3 %collective-permute-start.24 = (f32[1,4,96,1920]{3,2,1,0:T(8,128)}, f32[1,4,96,1920]{3,2,1,0:T(8,128)S(1)}, u32[]{:S(2)}, u32[]{:S(2)}) collective-permute-start(f32[1,4,96,1920]{3,2,1,0:T(8,128)} %dynamic-slice_bitcast_fusion), channel_id=1, source_target_pairs={{0,4},{4,0},{8,12},{12,8},{16,20},{20,16},{24,28},{28,24},{1,5},{5... | collective-permute-start | bytes 8847368 | tf_op jit(solution)/shard_map/ppermute | solution.py:678
  264.3 37.3 %collective-permute-start.26 = (f32[1,4,96,768]{3,2,1,0:T(8,128)}, f32[1,4,96,768]{3,2,1,0:T(8,128)}, u32[]{:S(2)}, u32[]{:S(2)}) collective-permute-start(f32[1,4,96,768]{3,2,1,0:T(8,128)} %dynamic-slice_bitcast_fusion.1), channel_id=1, source_target_pairs={{0,4},{4,0},{8,12},{12,8},{16,20},{20,16},{24,28},{28,24},{1,5},{5... | collective-permute-start | bytes 3538952 | tf_op jit(solution)/shard_map/ppermute | solution.py:678
  268.0 33.5 %collective-permute-start.25 = (f32[1,2,96,1920]{3,2,1,0:T(8,128)}, f32[1,2,96,1920]{3,2,1,0:T(8,128)}, u32[]{:S(2)}, u32[]{:S(2)}) collective-permute-start(f32[1,2,96,1920]{3,2,1,0:T(8,128)} %pad_maximum_fusion.4), channel_id=1, source_target_pairs={{0,8},{4,20},{8,0},{12,28},{16,24},{20,4},{24,16},{28,12},{1,9},{5... | collective-permute-start | bytes 4423688 | tf_op jit(solution)/shard_map/ppermute | solution.py:697
  269.8 31.8 %copy-start.1 = (f32[768,768]{1,0:T(8,128)S(1)}, f32[768,768]{1,0:T(8,128)}, u32[]{:S(2)}) copy-start(f32[768,768]{1,0:T(8,128)} %get-tuple-element.99) | copy-start | bytes 7077892
  304.0 33.9 %collective-permute-start.28 = (f32[1,2,96,768]{3,2,1,0:T(8,128)}, f32[1,2,96,768]{3,2,1,0:T(8,128)S(1)}, u32[]{:S(2)}, u32[]{:S(2)}) collective-permute-start(f32[1,2,96,768]{3,2,1,0:T(8,128)} %pad_maximum_fusion.10), channel_id=1, source_target_pairs={{0,8},{4,20},{8,0},{12,28},{16,24},{20,4},{24,16},{28,12},{1,9},{5... | collective-permute-start | bytes 1769480 | tf_op jit(solution)/shard_map/ppermute | solution.py:697
  305.9 32.0 %collective-permute-start.27 = (f32[1,96,1920]{2,1,0:T(8,128)S(1)}, f32[1,96,1920]{2,1,0:T(8,128)}, u32[]{:S(2)}, u32[]{:S(2)}) collective-permute-start(f32[1,96,1920]{2,1,0:T(8,128)S(1)} %dynamic-slice_bitcast_fusion.2), channel_id=1, source_target_pairs={{0,16},{4,12},{8,24},{12,4},{16,0},{20,28},{24,8},{28,20},{1,17},{... | collective-permute-start | bytes 2211848 | tf_op jit(solution)/shard_map/ppermute | solution.py:704
  339.3 6.8 %collective-permute-start.29 = (f32[1,96,768]{2,1,0:T(8,128)S(1)}, f32[1,96,768]{2,1,0:T(8,128)S(1)}, u32[]{:S(2)}, u32[]{:S(2)}) collective-permute-start(f32[1,96,768]{2,1,0:T(8,128)S(1)} %dynamic-slice_bitcast_fusion.3), channel_id=1, source_target_pairs={{0,16},{4,12},{8,24},{12,4},{16,0},{20,28},{24,8},{28,20},{1,17},{... | collective-permute-start | bytes 884744 | tf_op jit(solution)/shard_map/ppermute | solution.py:704
  (3 other events, 6.5 us)
